TPU v7x, 32 devices: a whole 2x2x4 slice. The times are simulated.
32 devices in a mesh: freq: 8 (over y, x, core), tile: 4 (over z).
Axes of the slice: x: 2, y: 2, z: 4, core: 2. Of those that a mesh axis runs over, the one named last changes fastest.
Arguments:
- source_field: float32 [2, 8, 64, 1024], P(None, 'freq', 'tile'), may hold values from -6 to 6
- receiver_field: float32 [2, 8, 64, 1024], P(None, 'freq', 'tile'), may hold values from -6 to 6
- velocity_store: float32 [8, 64, 1024], P('freq', 'tile'), may hold values from 0.5 to 1
- slice_owner: int32 [4], replicated, may hold values from 0 to 7, as said below
- region_map: int32 [64, 1024], P('tile', 'freq'), may hold values from 0 to 3, as said below
Outputs:
- wavefields: float32 [2, 2, 8, 64, 1024], P(None, None, 'freq', 'tile')
- smoothed_image: float32 [4, 64, 1024], P(None, 'tile', 'freq')
Inputs may be any that keep to these rules, and one draw needn't show every extreme that they name: `slice_owner`: the 4 entries are distinct stored-slice indices; slices 0 and 7 are always among them. `region_map`: labels along the second lateral dimension change at scattered cells.
All inputs are finite; a program needn't handle non-finite values.
Results may differ from a plain program's by a relative error of at most 0.000023.
Values sent between devices are 32-bit elements; how exact they have to be, the bound alone decides.
No kernel may reach another device: no remote copies, remote signals or barrier semaphores. Data moves between devices by JAX's collectives and lax.ppermute only.
A program may use at most 64 MiB of HBM per device.

v0:
```python
import functools
import math

import jax
import jax.numpy as jnp
from jax import lax
from jax.experimental import pallas as pl
from jax.experimental.pallas import tpu as pltpu
from jax.sharding import PartitionSpec as P


SWEEPS = 3
STEP_DEPTH = 4.0
SMOOTHING = 0.25
LANES = 128
SUB = 8
GAIN = 8.0


def tiled_rows(x):
    rows, columns = x.shape[-2:]
    lead = x.shape[:-2]
    x = x.reshape(lead + (rows // SUB, SUB, columns // LANES, LANES))
    return jnp.swapaxes(x, -3, -2).reshape(lead + (-1, LANES))


def untiled_rows(x, rows, columns):
    lead = x.shape[:-2]
    x = x.reshape(lead + (rows // SUB, columns // LANES, SUB, LANES))
    return jnp.swapaxes(x, -3, -2).reshape(lead + (rows, columns))


def tiled_row(r, slabs):
    return pl.ds((r // SUB) * SUB * slabs + r % SUB, slabs, stride=SUB)


def prepare_kernel(halo, owner, src, rcv, vel, lab, own, send_a, send_b, gather, wanted):
    _, rows, slabs, _ = own.shape
    me = lax.axis_index("freq")
    for d in range(wanted.shape[0]):
        wanted[d] = jnp.full(wanted.shape[1:], (owner[d] ^ me).astype(jnp.float32))
    for c in range(4):
        field = (src, rcv)[c // 2]
        for r in range(rows):
            own[c, r] = field[c % 2, tiled_row(r, slabs), :]
    even = lax.rem(lax.axis_index("tile"), 2) == 0
    a0 = jnp.where(even, rows - halo, 0)
    b0 = jnp.where(even, 0, rows - halo)
    for c in range(4):
        send_a[c] = own[c, pl.ds(a0, halo)]
        send_b[c] = own[c, pl.ds(b0, halo)]
    gather[: rows * slabs, :] = vel[...]
    gather[rows * slabs :, :] = lab[...].astype(jnp.float32)


def select_kernel(halos, starts, wanted, *refs):
    slices, (speeds, send_a, send_b) = refs[:-3], refs[-3:]
    _, rows, slabs, _ = speeds.shape
    even = lax.rem(lax.axis_index("tile"), 2) == 0
    for d, h in enumerate(halos):
        want = wanted[d, :slabs, :]
        hits = [want == float(k) for k in range(1, len(slices))]
        for r in range(rows):
            value = slices[0][tiled_row(r, slabs), :]
            for k, hit in enumerate(hits):
                value = jnp.where(hit, slices[k + 1][tiled_row(r, slabs), :], value)
            speeds[d, r] = value
        a0 = jnp.where(even, rows - h, 0)
        b0 = jnp.where(even, 0, rows - h)
        send_a[starts[d] : starts[d] + h] = speeds[d, pl.ds(a0, h)]
        send_b[starts[d] : starts[d] + h] = speeds[d, pl.ds(b0, h)]


def omega_here(freqs):
    return 1.0 + lax.axis_index("freq").astype(jnp.float32) * (1.0 / freqs)


def sin_cos(x):
    quarter = jnp.floor(x * (2.0 / math.pi) + 0.5)
    r = x - quarter * 1.5703125
    r = r - quarter * 4.837512969970703e-4
    r = r - quarter * 7.549789948768648e-8
    z = r * r
    s = r + r * z * (-1.6666654611e-1 + z * (8.3321608736e-3 - z * 1.9515295891e-4))
    c = 1.0 - 0.5 * z + z * z * (
        4.166664568298827e-2 + z * (-1.388731625493765e-3 + z * 2.443315711809948e-5)
    )
    q = quarter.astype(jnp.int32)
    odd = (q & 1) == 1
    sine = jnp.where(odd, c, s)
    cosine = jnp.where(odd, s, c)
    sine = jnp.where((q & 2) == 2, -sine, sine)
    cosine = jnp.where(((q + 1) & 2) == 2, -cosine, cosine)
    return sine, cosine


def depth_scale(d):
    return 1.0 if d == 0 else GAIN**-SWEEPS


def angles_kernel(freqs, speeds, labels, sines, cosines, ratios, keep_next, keep_prev, pad):
    depths, rows, slabs, _ = speeds.shape
    omega = omega_here(freqs)
    for d in range(depths):

        def row(i, carry, d=d):
            v = speeds[d, pl.ds(i * 4, 4)]
            s, c = sin_cos(omega * STEP_DEPTH / v)
            sines[d, pl.ds(i * 4, 4)] = s * depth_scale(d)
            cosines[d, pl.ds(i * 4, 4)] = c * depth_scale(d)
            ratios[d, pl.ds(i * 4, 4)] = v / omega
            return carry

        lax.fori_loop(0, rows // 4, row, 0, unroll=2)
    pad[...] = jnp.zeros_like(pad)
    mid = labels[...] + 1.0
    pad[:, SUB : SUB + slabs, :] = mid
    after, before = shifted(pad, slice(None))
    keep_next[...] = jnp.where(after == mid, SMOOTHING, 0.0)
    keep_prev[...] = jnp.where(before == mid, SMOOTHING, 0.0)


def shifted(pad, rows):
    slabs = pad.shape[-2] - 2 * SUB
    here = pad[rows, SUB : SUB + slabs, :]
    lane = lax.broadcasted_iota(jnp.int32, here.shape, 2)
    after = jnp.where(lane == 0, pad[rows, SUB + 1 : SUB + 1 + slabs, :], here)
    before = jnp.where(lane == LANES - 1, pad[rows, SUB - 1 : SUB - 1 + slabs, :], here)
    return pltpu.roll(after, LANES - 1, 2), pltpu.roll(before, 1, 2)


def march_kernel(
    freqs, tiles, halos, starts,
    own, field_a, field_b, speed_a, speed_b, sines, cosines, ratios, keep_next, keep_prev,
    waves, image,
    x, y, coef, term,
):
    _, rows, slabs, _ = own.shape
    depths = len(halos)
    halo = halos[0]
    high0 = halo + rows
    extent = high0 + halo
    mid = slice(SUB, SUB + slabs)
    tile = lax.axis_index("tile")
    even = lax.rem(tile, 2) == 0
    at_low = tile == 0
    at_high = tile == tiles - 1
    omega = omega_here(freqs)
    low_in = jnp.where(at_low, 0.0, 1.0)
    high_in = jnp.where(at_high, 0.0, 1.0)

    for buf in (x, y):
        for c in range(4):
            buf[c, :, :SUB, :] = jnp.zeros((extent, SUB, LANES), jnp.float32)
            buf[c, :, SUB + slabs :, :] = jnp.zeros((extent, SUB, LANES), jnp.float32)
    term[...] = jnp.zeros_like(term)

    def unpack(low, high):
        for c in range(4):
            y[c, 0:halo, mid, :] = low[c] * low_in
            y[c, high0:extent, mid, :] = high[c] * high_in

    @pl.when(even)
    def _():
        unpack(field_b, field_a)

    @pl.when(jnp.logical_not(even))
    def _():
        unpack(field_a, field_b)

    for c in range(4):
        y[c, halo:high0, mid, :] = own[c]

    def rotate(e, n, s, c):
        s0, s1, r0, r1 = (y[k, pl.ds(e, n), mid, :] for k in range(4))
        x[0, pl.ds(e, n), mid, :] = s0 * c - s1 * s
        x[1, pl.ds(e, n), mid, :] = s0 * s + s1 * c
        x[2, pl.ds(e, n), mid, :] = r0 * c + r1 * s
        x[3, pl.ds(e, n), mid, :] = r1 * c - r0 * s

    def sweep(src, dst, k):
        n = 2
        lo, hi = k, extent - k

        def chunk(e):
            ratio = coef[pl.ds(e, n)]
            for pair, sign in ((0, 1.0), (2, -1.0)):
                spread, total = [], []
                for c in (pair, pair + 1):
                    here = src.at[c]
                    q = here[pl.ds(e, n), mid, :] * 4.0
                    after, before = shifted(here, pl.ds(e, n))
                    around = (here[pl.ds(e + 1, n), mid, :] + here[pl.ds(e - 1, n), mid, :]) + (
                        after + before
                    )
                    spread.append(around - q)
                    total.append(around + q)
                if sign > 0:
                    first = total[0] - ratio * spread[1]
                    second = total[1] + ratio * spread[0]
                else:
                    first = total[0] + ratio * spread[1]
                    second = total[1] - ratio * spread[0]
                dst[pair, pl.ds(e, n), mid, :] = first
                dst[pair + 1, pl.ds(e, n), mid, :] = second

        for e in range(lo, hi, n):
            chunk(min(e, hi - n))
        for c in range(4):
            dst[c, halo - 1, mid, :] = dst[c, halo - 1, mid, :] * low_in
            dst[c, high0, mid, :] = dst[c, high0, mid, :] * high_in

    for d, h in enumerate(halos):
        scale = depth_scale(d)

        def halo_rows(i, carry, d=d, h=h, scale=scale):
            a = speed_a[starts[d] + i]
            b = speed_b[starts[d] + i]
            for low in (True, False):
                v = jnp.where(even, b, a) if low else jnp.where(even, a, b)
                v = jnp.where(at_low if low else at_high, 1.0, v)
                e = halo - h + i if low else high0 + i
                s, c = sin_cos(omega * STEP_DEPTH / v)
                coef[e] = v / omega
                rotate(e, 1, (s * scale)[None], (c * scale)[None])
            return carry

        lax.fori_loop(0, h, halo_rows, 0, unroll=3)

        def own_rows(i, carry, d=d):
            r = i * 4
            coef[pl.ds(halo + r, 4)] = ratios[d, pl.ds(r, 4)]
            rotate(halo + r, 4, sines[d, pl.ds(r, 4)], cosines[d, pl.ds(r, 4)])
            return carry

        lax.fori_loop(0, rows // 4, own_rows, 0, unroll=True)

        k = d * SWEEPS
        sweep(x, y, k + 1)
        sweep(y, x, k + 2)
        sweep(x, y, k + 3)

        norm = GAIN ** (-2 * SWEEPS) / math.sqrt(freqs)
        s0, s1, r0, r1 = (y[c, halo:high0, mid, :] for c in range(4))
        term[:, mid, :] = (s0 * r0 + s1 * r1) * norm
        here = term[:, mid, :]
        after, before = shifted(term, slice(None))
        smooth = here + (keep_next[...] * (after - here) + keep_prev[...] * (before - here))
        for r in range(rows):
            image[pl.ds(d * rows + r, slabs, stride=depths * rows), :] = smooth[r]

    for c in range(4):
        for r in range(rows):
            waves[c, tiled_row(r, slabs), :] = y[c, halo + r, mid, :] * GAIN**-SWEEPS


def swaps(freqs, tiles, first):
    pairs = []
    for t in range(tiles):
        u = t + 1 if (t - first) % 2 == 0 else t - 1
        for f in range(freqs):
            g = f
            if not 0 <= u < tiles:
                g = min(f ^ 1, freqs - 1)
            pairs.append((f * tiles + t, g * tiles + (u if 0 <= u < tiles else t)))
    return pairs


def from_all_freqs(x, freqs):
    if freqs & (freqs - 1):
        whole = lax.all_gather(x, "freq")
        me = lax.axis_index("freq")
        return [jnp.take(whole, jnp.minimum(me ^ k, freqs - 1), axis=0) for k in range(2 * freqs)]

    def swap(value, bits):
        return lax.ppermute(value, "freq", [(i, i ^ bits) for i in range(freqs)])

    near = [x]
    for k in range(2, freqs, 2):
        near.append(swap(x, k))
    return [v for x in near for v in (x, swap(x, 1))]


def sum_over_freqs(blocks, freqs):
    if freqs % 2 or freqs & (freqs - 1):
        return lax.psum_scatter(blocks, "freq", scatter_dimension=0, tiled=False)
    me = lax.axis_index("freq")
    core, chip = lax.rem(me, 2), me // 2

    def swap(value, bits):
        return lax.ppermute(value, "freq", [(i, i ^ bits) for i in range(freqs)])

    blocks = blocks.reshape((freqs // 2, 2) + blocks.shape[1:])
    kept = lax.dynamic_index_in_dim(blocks, core, 1, keepdims=False)
    sent = lax.dynamic_index_in_dim(blocks, 1 - core, 1, keepdims=False)
    kept = kept + swap(sent, 1)
    total = lax.dynamic_index_in_dim(kept, chip, 0, keepdims=False)
    others = []
    for m in range(1, freqs // 2):
        others.append(swap(lax.dynamic_index_in_dim(kept, chip ^ m, 0, keepdims=False), 2 * m))
    for other in others:
        total = total + other
    return total


def on_chip(x):
    return pltpu.with_memory_space_constraint(x, pltpu.VMEM)


def call(kernel, out, scratch=(), smem=0, operands=0):
    specs = [pl.BlockSpec(memory_space=pltpu.SMEM)] * smem
    specs += [pl.BlockSpec(memory_space=pltpu.VMEM)] * (operands - smem)
    return pl.pallas_call(
        kernel,
        out_shape=[pltpu.VMEM(s, jnp.float32) for s in out],
        in_specs=specs,
        out_specs=[pl.BlockSpec(memory_space=pltpu.VMEM)] * len(out),
        scratch_shapes=[pltpu.VMEM(s, jnp.float32) for s in scratch],
    )


def on_device(source_field, receiver_field, velocity_store, slice_owner, region_map):
    freqs, tiles = lax.axis_size("freq"), lax.axis_size("tile")
    _, _, rows, columns = source_field.shape
    slabs = columns // LANES
    depths = slice_owner.shape[0]
    halos = [SWEEPS * (depths - d) for d in range(depths)]
    starts = [sum(halos[:d]) for d in range(depths)]
    halo = halos[0]
    own_columns = region_map.shape[1]
    swap_a = functools.partial(lax.ppermute, axis_name=("freq", "tile"), perm=swaps(freqs, tiles, 0))
    swap_b = functools.partial(lax.ppermute, axis_name=("freq", "tile"), perm=swaps(freqs, tiles, 1))

    labels = region_map.reshape(-1, LANES)
    vel_rows = rows * slabs
    row = (slabs, LANES)
    own, send_a, send_b, gather, wanted = call(
        functools.partial(prepare_kernel, halo),
        [(4, rows) + row, (4, halo) + row, (4, halo) + row, (vel_rows + labels.shape[0], LANES), (depths, SUB, LANES)],
        smem=1,
        operands=5,
    )(
        slice_owner,
        tiled_rows(source_field[:, 0]),
        tiled_rows(receiver_field[:, 0]),
        tiled_rows(velocity_store[0]),
        labels,
    )
    field_a, field_b = swap_a(send_a), swap_b(send_b)
    gathered = from_all_freqs(gather, freqs)
    speeds, send_a, send_b = call(
        functools.partial(select_kernel, halos, starts),
        [(depths, rows) + row, (sum(halos),) + row, (sum(halos),) + row],
        operands=1 + len(gathered),
    )(on_chip(wanted), *map(on_chip, gathered))
    speed_a = swap_a(send_a)
    speed_b = swap_b(send_b)
    me = lax.axis_index("freq")
    labels = jnp.stack([x[vel_rows:, :] for x in gathered[:freqs]])
    labels = labels[jnp.arange(freqs, dtype=jnp.int32) ^ me].reshape(freqs, rows, own_columns)
    labels = jnp.swapaxes(labels, 0, 1).reshape((rows,) + row)
    table = (depths, rows) + row
    sines, cosines, ratios, keep_next, keep_prev = call(
        functools.partial(angles_kernel, freqs),
        [table, table, table, (rows,) + row, (rows,) + row],
        scratch=[(rows, slabs + 2 * SUB, LANES)],
        operands=2,
    )(on_chip(speeds), on_chip(labels))
    extent = rows + 2 * halo
    padded = (4, extent, slabs + 2 * SUB, LANES)
    waves, image = call(
        functools.partial(march_kernel, freqs, tiles, halos, starts),
        [(4, rows * slabs, LANES), (slabs * depths * rows, LANES)],
        scratch=[padded, padded, (extent,) + row, (rows, slabs + 2 * SUB, LANES)],
        operands=10,
    )(
        *map(
            on_chip,
            (own, field_a, field_b, speed_a, speed_b, sines, cosines, ratios, keep_next, keep_prev),
        )
    )

    if own_columns == LANES:
        blocks = image.reshape(freqs, depths * rows, LANES)
    else:
        blocks = jnp.swapaxes(image.reshape(slabs, depths * rows, LANES), 0, 1)
        blocks = blocks.reshape(depths * rows, freqs, own_columns)
        blocks = jnp.swapaxes(blocks, 0, 1)
    smoothed = sum_over_freqs(blocks, freqs).reshape(depths, rows, own_columns)
    waves = untiled_rows(waves, rows, columns).reshape(2, 2, 1, rows, columns)
    return waves, smoothed


def solution(mesh):
    in_specs = (
        P(None, "freq", "tile", None),
        P(None, "freq", "tile", None),
        P("freq", "tile", None),
        P(),
        P("tile", "freq"),
    )
    out_specs = (P(None, None, "freq", "tile", None), P(None, "tile", "freq"))

    return jax.shard_map(on_device, mesh=mesh, in_specs=in_specs, out_specs=out_specs, check_vma=False)
```

profile of v0, /device:TPU:0, one launch (start us, length us, event | category | flops | bytes accessed | tf_op | source)
XLA Modules:
  0.0 32.4 jit_solution(8313538728183807603)
XLA Ops:
  0.6 1.1 %shard_map.68 = (f32[4,16,8,128]{3,2,1,0:T(8,128)S(1)}, f32[4,12,8,128]{3,2,1,0:T(8,128)S(1)}, f32[4,12,8,128]{3,2,1,0:T(8,128)S(1)}, f32[144,128]{1,0:T(8,128)S(1)}, f32[4,8,128]{2,1,0:T(8,128)S(1)}) custom-call(s32[4]{0:T(128)} %owner.1, f32[2,128,128]{2,1,0:T(8,128)} %bitcast.77, f32[2,128,128]{2,1,0:T(8,128)} %bitcast.78, f32[128,128]{1,0:T(8,128)} %bitcast.79, ...), custom_call_target="tpu_custom_call" | custom-call | tf_op jit(solution)/shard_map/pallas_call | solution.py:337
  1.7 3.0 %collective-permute-start.3 = (f32[144,128]{1,0:T(8,128)S(1)}, f32[144,128]{1,0:T(8,128)S(1)}, u32[]{:S(2)}, u32[]{:S(2)}) collective-permute-start(f32[144,128]{1,0:T(8,128)S(1)} %get-tuple-element.21.refs_0_), channel_id=1, source_target_pairs={{0,8},{4,12},{8,0},{12,4},{16,24},{20,28},{24,16},{28,20},{1,9},{5... | collective-permute-start | bytes 221192 | tf_op jit(solution)/shard_map/ppermute | solution.py:276
  4.7 1.5 %collective-permute-start.5 = (f32[144,128]{1,0:T(8,128)S(1)}, f32[144,128]{1,0:T(8,128)S(1)}, u32[]{:S(2)}, u32[]{:S(2)}) collective-permute-start(f32[144,128]{1,0:T(8,128)S(1)} %get-tuple-element.21.refs_0_), channel_id=1, source_target_pairs={{0,16},{4,20},{8,24},{12,28},{16,0},{20,4},{24,8},{28,12},{1,17},{... | collective-permute-start | bytes 221192 | tf_op jit(solution)/shard_map/ppermute | solution.py:276
  6.3 0.0 collective-permute-start.7
  6.3 0.0 collective-permute-start.2
  6.3 2.0 %collective-permute-start = (f32[4,12,8,128]{3,2,1,0:T(8,128)S(1)}, f32[4,12,8,128]{3,2,1,0:T(8,128)S(1)}, u32[]{:S(2)}, u32[]{:S(2)}) collective-permute-start(f32[4,12,8,128]{3,2,1,0:T(8,128)S(1)} %get-tuple-element.18), channel_id=1, source_target_pairs={{0,1},{4,5},{8,9},{12,13},{16,17},{20,21},{24,25},{28,29},{1,0},{5... | collective-permute-start | bytes 589832 | tf_op jit(solution)/shard_map/ppermute | solution.py:349
  8.3 0.0 collective-permute-done.3.refs_2_
  8.3 0.3 collective-permute-start.1
  8.6 0.5 %collective-permute-done.5.refs_4_ = f32[144,128]{1,0:T(8,128)S(1)} collective-permute-done((f32[144,128]{1,0:T(8,128)S(1)}, f32[144,128]{1,0:T(8,128)S(1)}, u32[]{:S(2)}, u32[]{:S(2)}) %collective-permute-start.5) | collective-permute-done | bytes 73760 | tf_op jit(solution)/shard_map/ppermute | solution.py:276
  9.1 0.0 collective-permute-start.4
  9.1 2.4 %collective-permute-done.7.refs_6_ = f32[144,128]{1,0:T(8,128)S(1)} collective-permute-done((f32[144,128]{1,0:T(8,128)S(1)}, f32[144,128]{1,0:T(8,128)S(1)}, u32[]{:S(2)}, u32[]{:S(2)}) %collective-permute-start.7) | collective-permute-done | bytes 73760 | tf_op jit(solution)/shard_map/ppermute | solution.py:276
  11.5 0.0 collective-permute-start.6
  11.5 0.0 collective-permute-done.2.refs_1_
  11.5 0.5 %collective-permute-start.8 = (f32[144,128]{1,0:T(8,128)S(1)}, f32[144,128]{1,0:T(8,128)S(1)}, u32[]{:S(2)}, u32[]{:S(2)}) collective-permute-start(f32[144,128]{1,0:T(8,128)S(1)} %collective-permute-done.7.refs_6_), channel_id=1, source_target_pairs={{0,4},{4,0},{8,12},{12,8},{16,20},{20,16},{24,28},{28,24},{1,5},{5... | collective-permute-start | bytes 221192 | tf_op jit(solution)/shard_map/ppermute | solution.py:276
  12.0 0.0 collective-permute-done.4.refs_3_
  12.0 0.7 %collective-permute-done.6.refs_5_ = f32[144,128]{1,0:T(8,128)S(1)} collective-permute-done((f32[144,128]{1,0:T(8,128)S(1)}, f32[144,128]{1,0:T(8,128)S(1)}, u32[]{:S(2)}, u32[]{:S(2)}) %collective-permute-start.6) | collective-permute-done | bytes 73760 | tf_op jit(solution)/shard_map/ppermute | solution.py:276
  12.8 0.2 collective-permute-done.8.refs_7_
  12.9 0.3 shard_map.69
  13.3 0.4 %collective-permute-start.10 = (f32[30,8,128]{2,1,0:T(8,128)S(1)}, f32[30,8,128]{2,1,0:T(8,128)S(1)}, u32[]{:S(2)}, u32[]{:S(2)}) collective-permute-start(f32[30,8,128]{2,1,0:T(8,128)S(1)} %get-tuple-element.23), channel_id=1, source_target_pairs={{0,4},{4,0},{8,12},{12,8},{16,20},{20,16},{24,28},{28,24},{1,2},{5... | collective-permute-start | bytes 368648 | tf_op jit(solution)/shard_map/ppermute | solution.py:357
  13.7 2.8 %collective-permute-start.9 = (f32[30,8,128]{2,1,0:T(8,128)S(1)}, f32[30,8,128]{2,1,0:T(8,128)S(1)}, u32[]{:S(2)}, u32[]{:S(2)}) collective-permute-start(f32[30,8,128]{2,1,0:T(8,128)S(1)} %get-tuple-element.22), channel_id=1, source_target_pairs={{0,1},{4,5},{8,9},{12,13},{16,17},{20,21},{24,25},{28,29},{1,0},{5... | collective-permute-start | bytes 368648 | tf_op jit(solution)/shard_map/ppermute | solution.py:356
  16.5 0.6 %gather_fusion = f32[8,16,128]{2,1,0:T(8,128)S(1)} fusion(f32[8,16,128]{2,1,0:T(8,128)S(1)} %constant_dynamic-update-slice_fusion, s32[1024]{0:T(1024)S(1)} %pad_clamp_fusion), kind=kCustom, calls=%fused_computation | custom fusion | bytes 131104 | tf_op jit(solution)/shard_map/gather | solution.py:360
  17.1 0.6 %shard_map.70 = (f32[4,16,8,128]{3,2,1,0:T(8,128)S(1)}, f32[4,16,8,128]{3,2,1,0:T(8,128)S(1)}, f32[4,16,8,128]{3,2,1,0:T(8,128)S(1)}, f32[16,8,128]{2,1,0:T(8,128)S(1)}, f32[16,8,128]{2,1,0:T(8,128)S(1)}) custom-call(f32[4,16,8,128]{3,2,1,0:T(8,128)S(1)} %get-tuple-element.24.speeds, f32[16,8,128]{2,1,0:T(8,128)S(1)} %bitcast.74), custom_call_target="tpu_custom_call" | custom-call | tf_op jit(solution)/shard_map/pallas_call | solution.py:363
  17.7 0.0 collective-permute-done.field_a
  17.7 0.0 collective-permute-done.1.field_b
  17.7 0.0 collective-permute-done.10.speed_b
  17.7 2.3 %collective-permute-done.9.speed_a = f32[30,8,128]{2,1,0:T(8,128)S(1)} collective-permute-done((f32[30,8,128]{2,1,0:T(8,128)S(1)}, f32[30,8,128]{2,1,0:T(8,128)S(1)}, u32[]{:S(2)}, u32[]{:S(2)}) %collective-permute-start.9) | collective-permute-done | bytes 122912 | tf_op jit(solution)/shard_map/ppermute | solution.py:356
  20.0 4.1 %shard_map.71 = (f32[4,128,128]{2,1,0:T(8,128)S(1)}, f32[512,128]{1,0:T(8,128)S(1)}) custom-call(f32[4,16,8,128]{3,2,1,0:T(8,128)S(1)} %get-tuple-element.17.own, f32[4,12,8,128]{3,2,1,0:T(8,128)S(1)} %collective-permute-done.field_a, f32[4,12,8,128]{3,2,1,0:T(8,128)S(1)} %collective-permute-done.1.field_b, ...), custom_call_target="tpu_custom_call" | custom-call | tf_op jit(solution)/shard_map/pallas_call | solution.py:371
  24.2 0.1 collective-permute-start.11
  24.3 1.3 %collective-permute-done.11 = f32[4,64,128]{2,1,0:T(8,128)S(1)} collective-permute-done((f32[4,64,128]{2,1,0:T(8,128)S(1)}, f32[4,64,128]{2,1,0:T(8,128)S(1)}, u32[]{:S(2)}, u32[]{:S(2)}) %collective-permute-start.11) | collective-permute-done | bytes 131104 | tf_op jit(solution)/shard_map/ppermute | solution.py:291
  25.6 0.6 %collective-permute-start.12 = (f32[64,128]{1,0:T(8,128)S(1)}, f32[64,128]{1,0:T(8,128)S(1)}, u32[]{:S(2)}, u32[]{:S(2)}) collective-permute-start(f32[64,128]{1,0:T(8,128)S(1)} %get-tuple-element.32), channel_id=1, source_target_pairs={{0,8},{4,12},{8,0},{12,4},{16,24},{20,28},{24,16},{28,20},{1,9},{5... | collective-permute-start | bytes 98312 | tf_op jit(solution)/shard_map/ppermute | solution.py:291
  26.2 0.7 %collective-permute-start.13 = (f32[64,128]{1,0:T(8,128)S(1)}, f32[64,128]{1,0:T(8,128)S(1)}, u32[]{:S(2)}, u32[]{:S(2)}) collective-permute-start(f32[64,128]{1,0:T(8,128)S(1)} %get-tuple-element.34), channel_id=1, source_target_pairs={{0,16},{4,20},{8,24},{12,28},{16,0},{20,4},{24,8},{28,12},{1,17},{... | collective-permute-start | bytes 98312 | tf_op jit(solution)/shard_map/ppermute | solution.py:291
  26.9 2.3 %collective-permute-start.14 = (f32[64,128]{1,0:T(8,128)S(1)}, f32[64,128]{1,0:T(8,128)S(1)}, u32[]{:S(2)}, u32[]{:S(2)}) collective-permute-start(f32[64,128]{1,0:T(8,128)S(1)} %get-tuple-element.33), channel_id=1, source_target_pairs={{0,24},{4,28},{8,16},{12,20},{16,8},{20,12},{24,0},{28,4},{1,25},{... | collective-permute-start | bytes 98312 | tf_op jit(solution)/shard_map/ppermute | solution.py:291
  29.2 0.7 %copy.17 = f32[2,2,1,16,1024]{4,3,2,1,0:T(8,128)} copy(f32[2,2,1,16,1024]{4,3,2,1,0:T(8,128)S(1)} %bitcast.73) | data formatting | bytes 524288
  29.9 0.0 collective-permute-done.12
  29.9 0.6 %collective-permute-done.13 = f32[64,128]{1,0:T(8,128)S(1)} collective-permute-done((f32[64,128]{1,0:T(8,128)S(1)}, f32[64,128]{1,0:T(8,128)S(1)}, u32[]{:S(2)}, u32[]{:S(2)}) %collective-permute-start.13) | collective-permute-done | bytes 32800 | tf_op jit(solution)/shard_map/ppermute | solution.py:291
  30.5 1.2 %collective-permute-done.14 = f32[64,128]{1,0:T(8,128)S(1)} collective-permute-done((f32[64,128]{1,0:T(8,128)S(1)}, f32[64,128]{1,0:T(8,128)S(1)}, u32[]{:S(2)}, u32[]{:S(2)}) %collective-permute-start.14) | collective-permute-done | bytes 32800 | tf_op jit(solution)/shard_map/ppermute | solution.py:291
  31.7 0.6 %fusion.1 = f32[64,128]{1,0:T(8,128)} fusion(f32[64,128]{1,0:T(8,128)S(1)} %collective-permute-done.14, f32[64,128]{1,0:T(8,128)S(1)} %collective-permute-done.13, f32[64,128]{1,0:T(8,128)S(1)} %collective-permute-done.12, f32[4,64,128]{2,1,0:T(8,128)S(1)} %bitcast_add_fusion, s32[]{:T(128)S(6)} %select_n.39), kind=kLoop, calls=%fused_computation.6 | loop fusion | flops 24576 | bytes 163844 | tf_op jit(solution)/shard_map/add | solution.py:302
  (14 shorter events, 0.1 us)
Async XLA Ops:
  1.7 6.6 %collective-permute-start.3 = (f32[144,128]{1,0:T(8,128)S(1)}, f32[144,128]{1,0:T(8,128)S(1)}, u32[]{:S(2)}, u32[]{:S(2)}) collective-permute-start(f32[144,128]{1,0:T(8,128)S(1)} %get-tuple-element.21.refs_0_), channel_id=1, source_target_pairs={{0,8},{4,12},{8,0},{12,4},{16,24},{20,28},{24,16},{28,20},{1,9},{5... | collective-permute-start | bytes 221192 | tf_op jit(solution)/shard_map/ppermute | solution.py:276
  4.7 4.4 %collective-permute-start.5 = (f32[144,128]{1,0:T(8,128)S(1)}, f32[144,128]{1,0:T(8,128)S(1)}, u32[]{:S(2)}, u32[]{:S(2)}) collective-permute-start(f32[144,128]{1,0:T(8,128)S(1)} %get-tuple-element.21.refs_0_), channel_id=1, source_target_pairs={{0,16},{4,20},{8,24},{12,28},{16,0},{20,4},{24,8},{28,12},{1,17},{... | collective-permute-start | bytes 221192 | tf_op jit(solution)/shard_map/ppermute | solution.py:276
  6.3 5.3 %collective-permute-start.7 = (f32[144,128]{1,0:T(8,128)S(1)}, f32[144,128]{1,0:T(8,128)S(1)}, u32[]{:S(2)}, u32[]{:S(2)}) collective-permute-start(f32[144,128]{1,0:T(8,128)S(1)} %get-tuple-element.21.refs_0_), channel_id=1, source_target_pairs={{0,24},{4,28},{8,16},{12,20},{16,8},{20,12},{24,0},{28,4},{1,25},{... | collective-permute-start | bytes 221192 | tf_op jit(solution)/shard_map/ppermute | solution.py:276
  6.3 5.2 %collective-permute-start.2 = (f32[144,128]{1,0:T(8,128)S(1)}, f32[144,128]{1,0:T(8,128)S(1)}, u32[]{:S(2)}, u32[]{:S(2)}) collective-permute-start(f32[144,128]{1,0:T(8,128)S(1)} %get-tuple-element.21.refs_0_), channel_id=1, source_target_pairs={{0,4},{4,0},{8,12},{12,8},{16,20},{20,16},{24,28},{28,24},{1,5},{5... | collective-permute-start | bytes 221192 | tf_op jit(solution)/shard_map/ppermute | solution.py:276
  6.3 11.4 %collective-permute-start = (f32[4,12,8,128]{3,2,1,0:T(8,128)S(1)}, f32[4,12,8,128]{3,2,1,0:T(8,128)S(1)}, u32[]{:S(2)}, u32[]{:S(2)}) collective-permute-start(f32[4,12,8,128]{3,2,1,0:T(8,128)S(1)} %get-tuple-element.18), channel_id=1, source_target_pairs={{0,1},{4,5},{8,9},{12,13},{16,17},{20,21},{24,25},{28,29},{1,0},{5... | collective-permute-start | bytes 589832 | tf_op jit(solution)/shard_map/ppermute | solution.py:349
  8.3 9.4 %collective-permute-start.1 = (f32[4,12,8,128]{3,2,1,0:T(8,128)S(1)}, f32[4,12,8,128]{3,2,1,0:T(8,128)S(1)}, u32[]{:S(2)}, u32[]{:S(2)}) collective-permute-start(f32[4,12,8,128]{3,2,1,0:T(8,128)S(1)} %get-tuple-element.19), channel_id=1, source_target_pairs={{0,4},{4,0},{8,12},{12,8},{16,20},{20,16},{24,28},{28,24},{1,2},{5... | collective-permute-start | bytes 589832 | tf_op jit(solution)/shard_map/ppermute | solution.py:349
  9.1 2.9 %collective-permute-start.4 = (f32[144,128]{1,0:T(8,128)S(1)}, f32[144,128]{1,0:T(8,128)S(1)}, u32[]{:S(2)}, u32[]{:S(2)}) collective-permute-start(f32[144,128]{1,0:T(8,128)S(1)} %collective-permute-done.3.refs_2_), channel_id=1, source_target_pairs={{0,4},{4,0},{8,12},{12,8},{16,20},{20,16},{24,28},{28,24},{1,5},{5... | collective-permute-start | bytes 221192 | tf_op jit(solution)/shard_map/ppermute | solution.py:276
  11.5 1.3 %collective-permute-start.6 = (f32[144,128]{1,0:T(8,128)S(1)}, f32[144,128]{1,0:T(8,128)S(1)}, u32[]{:S(2)}, u32[]{:S(2)}) collective-permute-start(f32[144,128]{1,0:T(8,128)S(1)} %collective-permute-done.5.refs_4_), channel_id=1, source_target_pairs={{0,4},{4,0},{8,12},{12,8},{16,20},{20,16},{24,28},{28,24},{1,5},{5... | collective-permute-start | bytes 221192 | tf_op jit(solution)/shard_map/ppermute | solution.py:276
  11.5 1.4 %collective-permute-start.8 = (f32[144,128]{1,0:T(8,128)S(1)}, f32[144,128]{1,0:T(8,128)S(1)}, u32[]{:S(2)}, u32[]{:S(2)}) collective-permute-start(f32[144,128]{1,0:T(8,128)S(1)} %collective-permute-done.7.refs_6_), channel_id=1, source_target_pairs={{0,4},{4,0},{8,12},{12,8},{16,20},{20,16},{24,28},{28,24},{1,5},{5... | collective-permute-start | bytes 221192 | tf_op jit(solution)/shard_map/ppermute | solution.py:276
  13.3 4.4 %collective-permute-start.10 = (f32[30,8,128]{2,1,0:T(8,128)S(1)}, f32[30,8,128]{2,1,0:T(8,128)S(1)}, u32[]{:S(2)}, u32[]{:S(2)}) collective-permute-start(f32[30,8,128]{2,1,0:T(8,128)S(1)} %get-tuple-element.23), channel_id=1, source_target_pairs={{0,4},{4,0},{8,12},{12,8},{16,20},{20,16},{24,28},{28,24},{1,2},{5... | collective-permute-start | bytes 368648 | tf_op jit(solution)/shard_map/ppermute | solution.py:357
  13.7 6.4 %collective-permute-start.9 = (f32[30,8,128]{2,1,0:T(8,128)S(1)}, f32[30,8,128]{2,1,0:T(8,128)S(1)}, u32[]{:S(2)}, u32[]{:S(2)}) collective-permute-start(f32[30,8,128]{2,1,0:T(8,128)S(1)} %get-tuple-element.22), channel_id=1, source_target_pairs={{0,1},{4,5},{8,9},{12,13},{16,17},{20,21},{24,25},{28,29},{1,0},{5... | collective-permute-start | bytes 368648 | tf_op jit(solution)/shard_map/ppermute | solution.py:356
  24.2 1.4 %collective-permute-start.11 = (f32[4,64,128]{2,1,0:T(8,128)S(1)}, f32[4,64,128]{2,1,0:T(8,128)S(1)}, u32[]{:S(2)}, u32[]{:S(2)}) collective-permute-start(f32[4,64,128]{2,1,0:T(8,128)S(1)} %dynamic-slice_bitcast_fusion), channel_id=1, source_target_pairs={{0,4},{4,0},{8,12},{12,8},{16,20},{20,16},{24,28},{28,24},{1,5},{5... | collective-permute-start | bytes 393224 | tf_op jit(solution)/shard_map/ppermute | solution.py:291
  25.6 4.3 %collective-permute-start.12 = (f32[64,128]{1,0:T(8,128)S(1)}, f32[64,128]{1,0:T(8,128)S(1)}, u32[]{:S(2)}, u32[]{:S(2)}) collective-permute-start(f32[64,128]{1,0:T(8,128)S(1)} %get-tuple-element.32), channel_id=1, source_target_pairs={{0,8},{4,12},{8,0},{12,4},{16,24},{20,28},{24,16},{28,20},{1,9},{5... | collective-permute-start | bytes 98312 | tf_op jit(solution)/shard_map/ppermute | solution.py:291
  26.2 4.3 %collective-permute-start.13 = (f32[64,128]{1,0:T(8,128)S(1)}, f32[64,128]{1,0:T(8,128)S(1)}, u32[]{:S(2)}, u32[]{:S(2)}) collective-permute-start(f32[64,128]{1,0:T(8,128)S(1)} %get-tuple-element.34), channel_id=1, source_target_pairs={{0,16},{4,20},{8,24},{12,28},{16,0},{20,4},{24,8},{28,12},{1,17},{... | collective-permute-start | bytes 98312 | tf_op jit(solution)/shard_map/ppermute | solution.py:291
  26.9 4.8 %collective-permute-start.14 = (f32[64,128]{1,0:T(8,128)S(1)}, f32[64,128]{1,0:T(8,128)S(1)}, u32[]{:S(2)}, u32[]{:S(2)}) collective-permute-start(f32[64,128]{1,0:T(8,128)S(1)} %get-tuple-element.33), channel_id=1, source_target_pairs={{0,24},{4,28},{8,16},{12,20},{16,8},{20,12},{24,0},{28,4},{1,25},{... | collective-permute-start | bytes 98312 | tf_op jit(solution)/shard_map/ppermute | solution.py:291
where the time goes:
time: 32.5 us; the launch traced here: 32.4 us
  starting transfers between devices  14.3 us (44%)
  waiting for transfers between devices  9.26 us (28%)
  Pallas kernels  6.07 us (19%)
  local copies, waits for them, and re-layouts  1.33 us (4%)
  between operations  0.79 us (2%)
  other arithmetic  0.65 us (2%)
    ppermute x11, starting transfers between devices, swap(): return lax.ppermute(value, 'freq', [(i, i ^ bits) for i in range(freqs)])  8.71 us
    ppermute x11, waiting for transfers between devices, swap(): return lax.ppermute(value, 'freq', [(i, i ^ bits) for i in range(freqs)])  6.94 us
    pallas_call x1, Pallas kernels, on_device(): call(functools.partial(march_kernel, freqs, tiles, halos, starts), [(4, r...  4.1 us
    ppermute x1, starting transfers between devices, on_device(): speed_a = swap_a(send_a)  2.8 us
    ppermute x2, starting transfers between devices, on_device(): field_a, field_b = (swap_a(send_a), swap_b(send_b))  2.33 us
    ppermute x1, waiting for transfers between devices, on_device(): speed_a = swap_a(send_a)  2.32 us
    pallas_call x1, Pallas kernels, on_device(): call(functools.partial(prepare_kernel, halo), [(4, rows) + row, (4, halo)...  1.06 us
    unnamed x8, local copies, waits for them, and re-layouts  0.71 us
  transfers between devices with their start and end apart: 15, of which 8 were waited for; matrix products, arithmetic and copies ran while one was open for 4% of the time, Pallas kernels for 3%

commit v1 on v0

--- a/solution.py
+++ b/solution.py
@@ -15,6 +15,7 @@
 LANES = 128
 SUB = 8
 GAIN = 8.0
+VMEM_LIMIT = 24 * 2**20
 
 
 def tiled_rows(x):
@@ -129,13 +130,112 @@
     return pltpu.roll(after, LANES - 1, 2), pltpu.roll(before, 1, 2)
 
 
+def rotate(src, dst, e, n, s, c):
+    slabs = src.shape[-2] - 2 * SUB
+    mid = slice(SUB, SUB + slabs)
+    s0, s1, r0, r1 = (src[k, pl.ds(e, n), mid, :] for k in range(4))
+    dst[0, pl.ds(e, n), mid, :] = s0 * c - s1 * s
+    dst[1, pl.ds(e, n), mid, :] = s0 * s + s1 * c
+    dst[2, pl.ds(e, n), mid, :] = r0 * c + r1 * s
+    dst[3, pl.ds(e, n), mid, :] = r1 * c - r0 * s
+
+
+def sweep_rows(src, dst, ratio_of, lo, hi):
+    n = 2
+    slabs = src.shape[-2] - 2 * SUB
+    mid = slice(SUB, SUB + slabs)
+
+    def chunk(e):
+        ratio = ratio_of(e, n)
+        for pair, sign in ((0, 1.0), (2, -1.0)):
+            spread, total = [], []
+            for c in (pair, pair + 1):
+                here = src.at[c]
+                q = here[pl.ds(e, n), mid, :] * 4.0
+                after, before = shifted(here, pl.ds(e, n))
+                around = (here[pl.ds(e + 1, n), mid, :] + here[pl.ds(e - 1, n), mid, :]) + (
+                    after + before
+                )
+                spread.append(around - q)
+                total.append(around + q)
+            if sign > 0:
+                first = total[0] - ratio * spread[1]
+                second = total[1] + ratio * spread[0]
+            else:
+                first = total[0] + ratio * spread[1]
+                second = total[1] - ratio * spread[0]
+            dst[pair, pl.ds(e, n), mid, :] = first
+            dst[pair + 1, pl.ds(e, n), mid, :] = second
+
+    for e in range(lo, hi, n):
+        chunk(min(e, hi - n))
+
+
+def image_term(y, lo, hi, freqs):
+    slabs = y.shape[-2] - 2 * SUB
+    norm = GAIN ** (-2 * SWEEPS) / math.sqrt(freqs)
+    s0, s1, r0, r1 = (y[c, lo:hi, SUB : SUB + slabs, :] for c in range(4))
+    return (s0 * r0 + s1 * r1) * norm
+
+
+def begin_kernel(
+    freqs, tiles, halos, own, field_a, field_b, sines, cosines, ratios, x, y, z, early
+):
+    _, rows, slabs, _ = own.shape
+    halo = halos[0]
+    high0 = halo + rows
+    extent = high0 + halo
+    mid = slice(SUB, SUB + slabs)
+    tile = lax.axis_index("tile")
+    even = lax.rem(tile, 2) == 0
+    low_in = jnp.where(tile == 0, 0.0, 1.0)
+    high_in = jnp.where(tile == tiles - 1, 0.0, 1.0)
+
+    for buf in (x, y, z):
+        for c in range(4):
+            buf[c, :, :SUB, :] = jnp.zeros((extent, SUB, LANES), jnp.float32)
+            buf[c, :, SUB + slabs :, :] = jnp.zeros((extent, SUB, LANES), jnp.float32)
+
+    def unpack(low, high):
+        for c in range(4):
+            y[c, 0:halo, mid, :] = low[c] * low_in
+            y[c, high0:extent, mid, :] = high[c] * high_in
+
+    @pl.when(even)
+    def _():
+        unpack(field_b, field_a)
+
+    @pl.when(jnp.logical_not(even))
+    def _():
+        unpack(field_a, field_b)
+
+    for c in range(4):
+        y[c, halo:high0, mid, :] = own[c]
+
+    for d in range(len(halos)):
+        k = d * SWEEPS
+        turned = (x, z)[d % 2]
+        if 2 * k >= rows:
+            break
+        for r in range(k, rows - k, 2):
+            at = slice(r, r + 2)
+            rotate(y, turned, halo + r, 2, sines[d, at], cosines[d, at])
+        for src, dst in ((turned, y), (y, turned), (turned, y)):
+            k += 1
+            if 2 * k < rows:
+                ratio_of = lambda e, n, d=d: ratios[d, pl.ds(e - halo, n)]
+                sweep_rows(src, dst, ratio_of, halo + k, high0 - k)
+        if 2 * k < rows:
+            early[d, k : rows - k] = image_term(y, halo + k, high0 - k, freqs)
+
+
 def march_kernel(
     freqs, tiles, halos, starts,
-    own, field_a, field_b, speed_a, speed_b, sines, cosines, ratios, keep_next, keep_prev,
-    waves, image,
-    x, y, coef, term,
+    x_in, y_in, z_in, early, speed_a, speed_b, sines, cosines, ratios, keep_next, keep_prev,
+    x, y, z, waves, image,
+    coef, term,
 ):
-    _, rows, slabs, _ = own.shape
+    _, rows, slabs, _ = sines.shape
     depths = len(halos)
     halo = halos[0]
     high0 = halo + rows
@@ -148,72 +248,24 @@
     omega = omega_here(freqs)
     low_in = jnp.where(at_low, 0.0, 1.0)
     high_in = jnp.where(at_high, 0.0, 1.0)
-
-    for buf in (x, y):
-        for c in range(4):
-            buf[c, :, :SUB, :] = jnp.zeros((extent, SUB, LANES), jnp.float32)
-            buf[c, :, SUB + slabs :, :] = jnp.zeros((extent, SUB, LANES), jnp.float32)
     term[...] = jnp.zeros_like(term)
 
-    def unpack(low, high):
-        for c in range(4):
-            y[c, 0:halo, mid, :] = low[c] * low_in
-            y[c, high0:extent, mid, :] = high[c] * high_in
-
-    @pl.when(even)
-    def _():
-        unpack(field_b, field_a)
-
-    @pl.when(jnp.logical_not(even))
-    def _():
-        unpack(field_a, field_b)
-
-    for c in range(4):
-        y[c, halo:high0, mid, :] = own[c]
-
-    def rotate(e, n, s, c):
-        s0, s1, r0, r1 = (y[k, pl.ds(e, n), mid, :] for k in range(4))
-        x[0, pl.ds(e, n), mid, :] = s0 * c - s1 * s
-        x[1, pl.ds(e, n), mid, :] = s0 * s + s1 * c
-        x[2, pl.ds(e, n), mid, :] = r0 * c + r1 * s
-        x[3, pl.ds(e, n), mid, :] = r1 * c - r0 * s
-
     def sweep(src, dst, k):
-        n = 2
-        lo, hi = k, extent - k
-
-        def chunk(e):
-            ratio = coef[pl.ds(e, n)]
-            for pair, sign in ((0, 1.0), (2, -1.0)):
-                spread, total = [], []
-                for c in (pair, pair + 1):
-                    here = src.at[c]
-                    q = here[pl.ds(e, n), mid, :] * 4.0
-                    after, before = shifted(here, pl.ds(e, n))
-                    around = (here[pl.ds(e + 1, n), mid, :] + here[pl.ds(e - 1, n), mid, :]) + (
-                        after + before
-                    )
-                    spread.append(around - q)
-                    total.append(around + q)
-                if sign > 0:
-                    first = total[0] - ratio * spread[1]
-                    second = total[1] + ratio * spread[0]
-                else:
-                    first = total[0] + ratio * spread[1]
-                    second = total[1] - ratio * spread[0]
-                dst[pair, pl.ds(e, n), mid, :] = first
-                dst[pair + 1, pl.ds(e, n), mid, :] = second
-
-        for e in range(lo, hi, n):
-            chunk(min(e, hi - n))
+        ratio_of = lambda e, n: coef[pl.ds(e, n)]
+        if 2 * k < rows:
+            sweep_rows(src, dst, ratio_of, k, halo + k)
+            sweep_rows(src, dst, ratio_of, high0 - k, extent - k)
+        else:
+            sweep_rows(src, dst, ratio_of, k, extent - k)
         for c in range(4):
             dst[c, halo - 1, mid, :] = dst[c, halo - 1, mid, :] * low_in
             dst[c, high0, mid, :] = dst[c, high0, mid, :] * high_in
 
     for d, h in enumerate(halos):
         scale = depth_scale(d)
-
-        def halo_rows(i, carry, d=d, h=h, scale=scale):
+        turned = (x, z)[d % 2]
+
+        def halo_rows(i, carry, d=d, h=h, scale=scale, turned=turned):
             a = speed_a[starts[d] + i]
             b = speed_b[starts[d] + i]
             for low in (True, False):
@@ -222,27 +274,27 @@
                 e = halo - h + i if low else high0 + i
                 s, c = sin_cos(omega * STEP_DEPTH / v)
                 coef[e] = v / omega
-                rotate(e, 1, (s * scale)[None], (c * scale)[None])
+                rotate(y, turned, e, 1, (s * scale)[None], (c * scale)[None])
             return carry
 
         lax.fori_loop(0, h, halo_rows, 0, unroll=3)
-
-        def own_rows(i, carry, d=d):
-            r = i * 4
-            coef[pl.ds(halo + r, 4)] = ratios[d, pl.ds(r, 4)]
-            rotate(halo + r, 4, sines[d, pl.ds(r, 4)], cosines[d, pl.ds(r, 4)])
-            return carry
-
-        lax.fori_loop(0, rows // 4, own_rows, 0, unroll=True)
-
+        coef[halo:high0] = ratios[d]
         k = d * SWEEPS
-        sweep(x, y, k + 1)
-        sweep(y, x, k + 2)
-        sweep(x, y, k + 3)
-
-        norm = GAIN ** (-2 * SWEEPS) / math.sqrt(freqs)
-        s0, s1, r0, r1 = (y[c, halo:high0, mid, :] for c in range(4))
-        term[:, mid, :] = (s0 * r0 + s1 * r1) * norm
+        for r in range(rows):
+            if r < k or r >= rows - k:
+                rotate(y, turned, halo + r, 1, sines[d, r : r + 1], cosines[d, r : r + 1])
+
+        sweep(turned, y, k + 1)
+        sweep(y, turned, k + 2)
+        sweep(turned, y, k + 3)
+
+        k += SWEEPS
+        if 2 * k < rows:
+            term[:k, mid, :] = image_term(y, halo, halo + k, freqs)
+            term[k : rows - k, mid, :] = early[d, k : rows - k]
+            term[rows - k :, mid, :] = image_term(y, high0 - k, high0, freqs)
+        else:
+            term[:, mid, :] = image_term(y, halo, high0, freqs)
         here = term[:, mid, :]
         after, before = shifted(term, slice(None))
         smooth = here + (keep_next[...] * (after - here) + keep_prev[...] * (before - here))
@@ -307,7 +359,7 @@
     return pltpu.with_memory_space_constraint(x, pltpu.VMEM)
 
 
-def call(kernel, out, scratch=(), smem=0, operands=0):
+def call(kernel, out, scratch=(), name=None, smem=0, operands=0, aliases=None):
     specs = [pl.BlockSpec(memory_space=pltpu.SMEM)] * smem
     specs += [pl.BlockSpec(memory_space=pltpu.VMEM)] * (operands - smem)
     return pl.pallas_call(
@@ -316,6 +368,8 @@
         in_specs=specs,
         out_specs=[pl.BlockSpec(memory_space=pltpu.VMEM)] * len(out),
         scratch_shapes=[pltpu.VMEM(s, jnp.float32) for s in scratch],
+        input_output_aliases=aliases or {},
+        compiler_params=None if name == 'prepare' else pltpu.CompilerParams(vmem_limit_bytes=VMEM_LIMIT),
     )
 
 
@@ -339,6 +393,7 @@
         [(4, rows) + row, (4, halo) + row, (4, halo) + row, (vel_rows + labels.shape[0], LANES), (depths, SUB, LANES)],
         smem=1,
         operands=5,
+        name="prepare",
     )(
         slice_owner,
         tiled_rows(source_field[:, 0]),
@@ -352,6 +407,7 @@
         functools.partial(select_kernel, halos, starts),
         [(depths, rows) + row, (sum(halos),) + row, (sum(halos),) + row],
         operands=1 + len(gathered),
+        name="select",
     )(on_chip(wanted), *map(on_chip, gathered))
     speed_a = swap_a(send_a)
     speed_b = swap_b(send_b)
@@ -365,18 +421,27 @@
         [table, table, table, (rows,) + row, (rows,) + row],
         scratch=[(rows, slabs + 2 * SUB, LANES)],
         operands=2,
+        name="angles",
     )(on_chip(speeds), on_chip(labels))
     extent = rows + 2 * halo
     padded = (4, extent, slabs + 2 * SUB, LANES)
-    waves, image = call(
+    x, y, z, early = call(
+        functools.partial(begin_kernel, freqs, tiles, halos),
+        [padded] * 3 + [table],
+        operands=6,
+        name="begin",
+    )(*map(on_chip, (own, field_a, field_b, sines, cosines, ratios)))
+    _, _, _, waves, image = call(
         functools.partial(march_kernel, freqs, tiles, halos, starts),
-        [(4, rows * slabs, LANES), (slabs * depths * rows, LANES)],
-        scratch=[padded, padded, (extent,) + row, (rows, slabs + 2 * SUB, LANES)],
-        operands=10,
+        [padded] * 3 + [(4, rows * slabs, LANES), (slabs * depths * rows, LANES)],
+        scratch=[(extent,) + row, (rows, slabs + 2 * SUB, LANES)],
+        operands=11,
+        aliases={0: 0, 1: 1, 2: 2},
+        name="march",
     )(
         *map(
             on_chip,
-            (own, field_a, field_b, speed_a, speed_b, sines, cosines, ratios, keep_next, keep_prev),
+            (x, y, z, early, speed_a, speed_b, sines, cosines, ratios, keep_next, keep_prev),
         )
     )
 

time: 32.5 us -> 31.8 us (0.978)
  waiting for transfers between devices: 9.26 us -> 8.23 us
  Pallas kernels: 6.07 us -> 6.43 us
    ppermute x1, waiting for transfers between devices: 2.32 us -> 1.29 us  [on_device(): speed_a = swap_a(send_a)]
    pallas_call x1 -> x2, Pallas kernels: 4.1 us -> 4.46 us  [the longest x1 3.44 us: on_device(): call(functools.partial(march_kernel, freqs, tiles, halos, starts), [padde...]
  transfers between devices with their start and end apart: 15 -> 15, of which waited for: 8 -> 8; matrix products, arithmetic and copies ran while one was open for 4% -> 4% of each run, Pallas kernels for 3% -> 6%
where the time goes in v1:
time: 31.8 us; the launch traced here: 31.7 us
  starting transfers between devices  14.3 us (45%)
  waiting for transfers between devices  8.23 us (26%)
  Pallas kernels  6.43 us (20%)
  local copies, waits for them, and re-layouts  1.33 us (4%)
  between operations  0.8 us (3%)
  other arithmetic  0.65 us (2%)
    ppermute x11, starting transfers between devices, swap(): return lax.ppermute(value, 'freq', [(i, i ^ bits) for i in range(freqs)])  8.71 us
    ppermute x11, waiting for transfers between devices, swap(): return lax.ppermute(value, 'freq', [(i, i ^ bits) for i in range(freqs)])  6.94 us
    pallas_call x1, Pallas kernels, on_device(): call(functools.partial(march_kernel, freqs, tiles, halos, starts), [padde...  3.44 us
    ppermute x1, starting transfers between devices, on_device(): speed_a = swap_a(send_a)  2.8 us
    ppermute x2, starting transfers between devices, on_device(): field_a, field_b = (swap_a(send_a), swap_b(send_b))  2.33 us
    ppermute x1, waiting for transfers between devices, on_device(): speed_a = swap_a(send_a)  1.29 us
    pallas_call x1, Pallas kernels, on_device(): call(functools.partial(prepare_kernel, halo), [(4, rows) + row, (4, halo)...  1.06 us
    pallas_call x1, Pallas kernels, on_device(): call(functools.partial(begin_kernel, freqs, tiles, halos), [padded] * 3 +...  1.02 us
  transfers between devices with their start and end apart: 15, of which 8 were waited for; matrix products, arithmetic and copies ran while one was open for 4% of the time, Pallas kernels for 6%

profile of v1, /device:TPU:0, one launch (start us, length us, event | category | flops | bytes accessed | tf_op | source)
XLA Modules:
  0.0 31.7 jit_solution(870872721228407061)
XLA Ops:
  0.6 1.1 %shard_map.68 = (f32[4,16,8,128]{3,2,1,0:T(8,128)S(1)}, f32[4,12,8,128]{3,2,1,0:T(8,128)S(1)}, f32[4,12,8,128]{3,2,1,0:T(8,128)S(1)}, f32[144,128]{1,0:T(8,128)S(1)}, f32[4,8,128]{2,1,0:T(8,128)S(1)}) custom-call(s32[4]{0:T(128)} %owner.1, f32[2,128,128]{2,1,0:T(8,128)} %bitcast.77, f32[2,128,128]{2,1,0:T(8,128)} %bitcast.78, f32[128,128]{1,0:T(8,128)} %bitcast.79, ...), custom_call_target="tpu_custom_call" | custom-call | tf_op jit(solution)/shard_map/pallas_call | solution.py:391
  1.7 3.0 %collective-permute-start.3 = (f32[144,128]{1,0:T(8,128)S(1)}, f32[144,128]{1,0:T(8,128)S(1)}, u32[]{:S(2)}, u32[]{:S(2)}) collective-permute-start(f32[144,128]{1,0:T(8,128)S(1)} %get-tuple-element.25.refs_0_), channel_id=1, source_target_pairs={{0,8},{4,12},{8,0},{12,4},{16,24},{20,28},{24,16},{28,20},{1,9},{5... | collective-permute-start | bytes 221192 | tf_op jit(solution)/shard_map/ppermute | solution.py:328
  4.7 1.5 %collective-permute-start.5 = (f32[144,128]{1,0:T(8,128)S(1)}, f32[144,128]{1,0:T(8,128)S(1)}, u32[]{:S(2)}, u32[]{:S(2)}) collective-permute-start(f32[144,128]{1,0:T(8,128)S(1)} %get-tuple-element.25.refs_0_), channel_id=1, source_target_pairs={{0,16},{4,20},{8,24},{12,28},{16,0},{20,4},{24,8},{28,12},{1,17},{... | collective-permute-start | bytes 221192 | tf_op jit(solution)/shard_map/ppermute | solution.py:328
  6.3 0.0 collective-permute-start.7
  6.3 0.0 collective-permute-start.2
  6.3 2.0 %collective-permute-start = (f32[4,12,8,128]{3,2,1,0:T(8,128)S(1)}, f32[4,12,8,128]{3,2,1,0:T(8,128)S(1)}, u32[]{:S(2)}, u32[]{:S(2)}) collective-permute-start(f32[4,12,8,128]{3,2,1,0:T(8,128)S(1)} %get-tuple-element.22), channel_id=1, source_target_pairs={{0,1},{4,5},{8,9},{12,13},{16,17},{20,21},{24,25},{28,29},{1,0},{5... | collective-permute-start | bytes 589832 | tf_op jit(solution)/shard_map/ppermute | solution.py:404
  8.3 0.0 collective-permute-done.3.refs_2_
  8.3 0.3 collective-permute-start.1
  8.6 0.5 %collective-permute-done.5.refs_4_ = f32[144,128]{1,0:T(8,128)S(1)} collective-permute-done((f32[144,128]{1,0:T(8,128)S(1)}, f32[144,128]{1,0:T(8,128)S(1)}, u32[]{:S(2)}, u32[]{:S(2)}) %collective-permute-start.5) | collective-permute-done | bytes 73760 | tf_op jit(solution)/shard_map/ppermute | solution.py:328
  9.1 0.0 collective-permute-start.4
  9.1 2.4 %collective-permute-done.7.refs_6_ = f32[144,128]{1,0:T(8,128)S(1)} collective-permute-done((f32[144,128]{1,0:T(8,128)S(1)}, f32[144,128]{1,0:T(8,128)S(1)}, u32[]{:S(2)}, u32[]{:S(2)}) %collective-permute-start.7) | collective-permute-done | bytes 73760 | tf_op jit(solution)/shard_map/ppermute | solution.py:328
  11.5 0.0 collective-permute-start.6
  11.5 0.0 collective-permute-done.2.refs_1_
  11.5 0.5 %collective-permute-start.8 = (f32[144,128]{1,0:T(8,128)S(1)}, f32[144,128]{1,0:T(8,128)S(1)}, u32[]{:S(2)}, u32[]{:S(2)}) collective-permute-start(f32[144,128]{1,0:T(8,128)S(1)} %collective-permute-done.7.refs_6_), channel_id=1, source_target_pairs={{0,4},{4,0},{8,12},{12,8},{16,20},{20,16},{24,28},{28,24},{1,5},{5... | collective-permute-start | bytes 221192 | tf_op jit(solution)/shard_map/ppermute | solution.py:328
  12.0 0.0 collective-permute-done.4.refs_3_
  12.0 0.7 %collective-permute-done.6.refs_5_ = f32[144,128]{1,0:T(8,128)S(1)} collective-permute-done((f32[144,128]{1,0:T(8,128)S(1)}, f32[144,128]{1,0:T(8,128)S(1)}, u32[]{:S(2)}, u32[]{:S(2)}) %collective-permute-start.6) | collective-permute-done | bytes 73760 | tf_op jit(solution)/shard_map/ppermute | solution.py:328
  12.8 0.2 collective-permute-done.8.refs_7_
  12.9 0.3 %shard_map.69 = (f32[4,16,8,128]{3,2,1,0:T(8,128)S(1)}, f32[30,8,128]{2,1,0:T(8,128)S(1)}, f32[30,8,128]{2,1,0:T(8,128)S(1)}) custom-call(f32[4,8,128]{2,1,0:T(8,128)S(1)} %get-tuple-element.24.wanted, f32[144,128]{1,0:T(8,128)S(1)} %get-tuple-element.25.refs_0_, f32[144,128]{1,0:T(8,128)S(1)} %collective-permute-done.2.refs_1_, ...), custom_call_target="tpu_custom_call" | custom-call | tf_op jit(solution)/shard_map/pallas_call | solution.py:406
  13.3 0.4 %collective-permute-start.10 = (f32[30,8,128]{2,1,0:T(8,128)S(1)}, f32[30,8,128]{2,1,0:T(8,128)S(1)}, u32[]{:S(2)}, u32[]{:S(2)}) collective-permute-start(f32[30,8,128]{2,1,0:T(8,128)S(1)} %get-tuple-element.35), channel_id=1, source_target_pairs={{0,4},{4,0},{8,12},{12,8},{16,20},{20,16},{24,28},{28,24},{1,2},{5... | collective-permute-start | bytes 368648 | tf_op jit(solution)/shard_map/ppermute | solution.py:413
  13.7 2.8 %collective-permute-start.9 = (f32[30,8,128]{2,1,0:T(8,128)S(1)}, f32[30,8,128]{2,1,0:T(8,128)S(1)}, u32[]{:S(2)}, u32[]{:S(2)}) collective-permute-start(f32[30,8,128]{2,1,0:T(8,128)S(1)} %get-tuple-element.34), channel_id=1, source_target_pairs={{0,1},{4,5},{8,9},{12,13},{16,17},{20,21},{24,25},{28,29},{1,0},{5... | collective-permute-start | bytes 368648 | tf_op jit(solution)/shard_map/ppermute | solution.py:412
  16.5 0.6 %gather_fusion = f32[8,16,128]{2,1,0:T(8,128)S(1)} fusion(f32[8,16,128]{2,1,0:T(8,128)S(1)} %constant_dynamic-update-slice_fusion, s32[1024]{0:T(1024)S(1)} %pad_clamp_fusion), kind=kCustom, calls=%fused_computation | custom fusion | bytes 131104 | tf_op jit(solution)/shard_map/gather | solution.py:416
  17.1 0.6 %shard_map.70 = (f32[4,16,8,128]{3,2,1,0:T(8,128)S(1)}, f32[4,16,8,128]{3,2,1,0:T(8,128)S(1)}, f32[4,16,8,128]{3,2,1,0:T(8,128)S(1)}, f32[16,8,128]{2,1,0:T(8,128)S(1)}, f32[16,8,128]{2,1,0:T(8,128)S(1)}) custom-call(f32[4,16,8,128]{3,2,1,0:T(8,128)S(1)} %get-tuple-element.26.speeds, f32[16,8,128]{2,1,0:T(8,128)S(1)} %bitcast.74), custom_call_target="tpu_custom_call" | custom-call | tf_op jit(solution)/shard_map/pallas_call | solution.py:419
  17.7 0.0 collective-permute-done.field_a
  17.7 0.0 collective-permute-done.1.field_b
  17.7 1.0 %shard_map.71 = (f32[4,40,24,128]{3,2,1,0:T(8,128)S(1)}, f32[4,40,24,128]{3,2,1,0:T(8,128)S(1)}, f32[4,40,24,128]{3,2,1,0:T(8,128)S(1)}, f32[4,16,8,128]{3,2,1,0:T(8,128)S(1)}) custom-call(f32[4,16,8,128]{3,2,1,0:T(8,128)S(1)} %get-tuple-element.21.own, f32[4,12,8,128]{3,2,1,0:T(8,128)S(1)} %collective-permute-done.field_a, ...), custom_call_target="tpu_custom_call" | custom-call | tf_op jit(solution)/shard_map/pallas_call | solution.py:428
  18.7 0.0 collective-permute-done.10.speed_b
  18.7 1.3 %collective-permute-done.9.speed_a = f32[30,8,128]{2,1,0:T(8,128)S(1)} collective-permute-done((f32[30,8,128]{2,1,0:T(8,128)S(1)}, f32[30,8,128]{2,1,0:T(8,128)S(1)}, u32[]{:S(2)}, u32[]{:S(2)}) %collective-permute-start.9) | collective-permute-done | bytes 122912 | tf_op jit(solution)/shard_map/ppermute | solution.py:412
  20.0 3.4 %shard_map.72 = (f32[4,40,24,128]{3,2,1,0:T(8,128)S(1)}, f32[4,40,24,128]{3,2,1,0:T(8,128)S(1)}, f32[4,40,24,128]{3,2,1,0:T(8,128)S(1)}, f32[4,128,128]{2,1,0:T(8,128)S(1)}, f32[512,128]{1,0:T(8,128)S(1)}) custom-call(f32[4,40,24,128]{3,2,1,0:T(8,128)S(1)} %get-tuple-element.30.x_in, ...), custom_call_target="tpu_custom_call", output_to_operand_aliasing={{0}: (0, {}), {1}: (1, {}), {2}: (2, {})} | custom-call | tf_op jit(solution)/shard_map/pallas_call | solution.py:434
  23.5 0.1 collective-permute-start.11
  23.6 1.3 %collective-permute-done.11 = f32[4,64,128]{2,1,0:T(8,128)S(1)} collective-permute-done((f32[4,64,128]{2,1,0:T(8,128)S(1)}, f32[4,64,128]{2,1,0:T(8,128)S(1)}, u32[]{:S(2)}, u32[]{:S(2)}) %collective-permute-start.11) | collective-permute-done | bytes 131104 | tf_op jit(solution)/shard_map/ppermute | solution.py:343
  25.0 0.6 %collective-permute-start.12 = (f32[64,128]{1,0:T(8,128)S(1)}, f32[64,128]{1,0:T(8,128)S(1)}, u32[]{:S(2)}, u32[]{:S(2)}) collective-permute-start(f32[64,128]{1,0:T(8,128)S(1)} %get-tuple-element.40), channel_id=1, source_target_pairs={{0,8},{4,12},{8,0},{12,4},{16,24},{20,28},{24,16},{28,20},{1,9},{5... | collective-permute-start | bytes 98312 | tf_op jit(solution)/shard_map/ppermute | solution.py:343
  25.6 0.7 %collective-permute-start.13 = (f32[64,128]{1,0:T(8,128)S(1)}, f32[64,128]{1,0:T(8,128)S(1)}, u32[]{:S(2)}, u32[]{:S(2)}) collective-permute-start(f32[64,128]{1,0:T(8,128)S(1)} %get-tuple-element.42), channel_id=1, source_target_pairs={{0,16},{4,20},{8,24},{12,28},{16,0},{20,4},{24,8},{28,12},{1,17},{... | collective-permute-start | bytes 98312 | tf_op jit(solution)/shard_map/ppermute | solution.py:343
  26.3 2.3 %collective-permute-start.14 = (f32[64,128]{1,0:T(8,128)S(1)}, f32[64,128]{1,0:T(8,128)S(1)}, u32[]{:S(2)}, u32[]{:S(2)}) collective-permute-start(f32[64,128]{1,0:T(8,128)S(1)} %get-tuple-element.41), channel_id=1, source_target_pairs={{0,24},{4,28},{8,16},{12,20},{16,8},{20,12},{24,0},{28,4},{1,25},{... | collective-permute-start | bytes 98312 | tf_op jit(solution)/shard_map/ppermute | solution.py:343
  28.5 0.7 %copy.23 = f32[2,2,1,16,1024]{4,3,2,1,0:T(8,128)} copy(f32[2,2,1,16,1024]{4,3,2,1,0:T(8,128)S(1)} %bitcast.73) | data formatting | bytes 524288
  29.2 0.0 collective-permute-done.12
  29.2 0.6 %collective-permute-done.13 = f32[64,128]{1,0:T(8,128)S(1)} collective-permute-done((f32[64,128]{1,0:T(8,128)S(1)}, f32[64,128]{1,0:T(8,128)S(1)}, u32[]{:S(2)}, u32[]{:S(2)}) %collective-permute-start.13) | collective-permute-done | bytes 32800 | tf_op jit(solution)/shard_map/ppermute | solution.py:343
  29.8 1.2 %collective-permute-done.14 = f32[64,128]{1,0:T(8,128)S(1)} collective-permute-done((f32[64,128]{1,0:T(8,128)S(1)}, f32[64,128]{1,0:T(8,128)S(1)}, u32[]{:S(2)}, u32[]{:S(2)}) %collective-permute-start.14) | collective-permute-done | bytes 32800 | tf_op jit(solution)/shard_map/ppermute | solution.py:343
  31.1 0.6 %fusion.1 = f32[64,128]{1,0:T(8,128)} fusion(f32[64,128]{1,0:T(8,128)S(1)} %collective-permute-done.14, f32[64,128]{1,0:T(8,128)S(1)} %collective-permute-done.13, f32[64,128]{1,0:T(8,128)S(1)} %collective-permute-done.12, f32[4,64,128]{2,1,0:T(8,128)S(1)} %bitcast_add_fusion, s32[]{:T(128)S(6)} %select_n.39), kind=kLoop, calls=%fused_computation.6 | loop fusion | flops 24576 | bytes 163844 | tf_op jit(solution)/shard_map/add | solution.py:354
  (14 shorter events, 0.1 us)
Async XLA Ops:
  1.7 6.6 %collective-permute-start.3 = (f32[144,128]{1,0:T(8,128)S(1)}, f32[144,128]{1,0:T(8,128)S(1)}, u32[]{:S(2)}, u32[]{:S(2)}) collective-permute-start(f32[144,128]{1,0:T(8,128)S(1)} %get-tuple-element.25.refs_0_), channel_id=1, source_target_pairs={{0,8},{4,12},{8,0},{12,4},{16,24},{20,28},{24,16},{28,20},{1,9},{5... | collective-permute-start | bytes 221192 | tf_op jit(solution)/shard_map/ppermute | solution.py:328
  4.7 4.4 %collective-permute-start.5 = (f32[144,128]{1,0:T(8,128)S(1)}, f32[144,128]{1,0:T(8,128)S(1)}, u32[]{:S(2)}, u32[]{:S(2)}) collective-permute-start(f32[144,128]{1,0:T(8,128)S(1)} %get-tuple-element.25.refs_0_), channel_id=1, source_target_pairs={{0,16},{4,20},{8,24},{12,28},{16,0},{20,4},{24,8},{28,12},{1,17},{... | collective-permute-start | bytes 221192 | tf_op jit(solution)/shard_map/ppermute | solution.py:328
  6.3 5.3 %collective-permute-start.7 = (f32[144,128]{1,0:T(8,128)S(1)}, f32[144,128]{1,0:T(8,128)S(1)}, u32[]{:S(2)}, u32[]{:S(2)}) collective-permute-start(f32[144,128]{1,0:T(8,128)S(1)} %get-tuple-element.25.refs_0_), channel_id=1, source_target_pairs={{0,24},{4,28},{8,16},{12,20},{16,8},{20,12},{24,0},{28,4},{1,25},{... | collective-permute-start | bytes 221192 | tf_op jit(solution)/shard_map/ppermute | solution.py:328
  6.3 5.2 %collective-permute-start.2 = (f32[144,128]{1,0:T(8,128)S(1)}, f32[144,128]{1,0:T(8,128)S(1)}, u32[]{:S(2)}, u32[]{:S(2)}) collective-permute-start(f32[144,128]{1,0:T(8,128)S(1)} %get-tuple-element.25.refs_0_), channel_id=1, source_target_pairs={{0,4},{4,0},{8,12},{12,8},{16,20},{20,16},{24,28},{28,24},{1,5},{5... | collective-permute-start | bytes 221192 | tf_op jit(solution)/shard_map/ppermute | solution.py:328
  6.3 11.4 %collective-permute-start = (f32[4,12,8,128]{3,2,1,0:T(8,128)S(1)}, f32[4,12,8,128]{3,2,1,0:T(8,128)S(1)}, u32[]{:S(2)}, u32[]{:S(2)}) collective-permute-start(f32[4,12,8,128]{3,2,1,0:T(8,128)S(1)} %get-tuple-element.22), channel_id=1, source_target_pairs={{0,1},{4,5},{8,9},{12,13},{16,17},{20,21},{24,25},{28,29},{1,0},{5... | collective-permute-start | bytes 589832 | tf_op jit(solution)/shard_map/ppermute | solution.py:404
  8.3 9.4 %collective-permute-start.1 = (f32[4,12,8,128]{3,2,1,0:T(8,128)S(1)}, f32[4,12,8,128]{3,2,1,0:T(8,128)S(1)}, u32[]{:S(2)}, u32[]{:S(2)}) collective-permute-start(f32[4,12,8,128]{3,2,1,0:T(8,128)S(1)} %get-tuple-element.23), channel_id=1, source_target_pairs={{0,4},{4,0},{8,12},{12,8},{16,20},{20,16},{24,28},{28,24},{1,2},{5... | collective-permute-start | bytes 589832 | tf_op jit(solution)/shard_map/ppermute | solution.py:404
  9.1 2.9 %collective-permute-start.4 = (f32[144,128]{1,0:T(8,128)S(1)}, f32[144,128]{1,0:T(8,128)S(1)}, u32[]{:S(2)}, u32[]{:S(2)}) collective-permute-start(f32[144,128]{1,0:T(8,128)S(1)} %collective-permute-done.3.refs_2_), channel_id=1, source_target_pairs={{0,4},{4,0},{8,12},{12,8},{16,20},{20,16},{24,28},{28,24},{1,5},{5... | collective-permute-start | bytes 221192 | tf_op jit(solution)/shard_map/ppermute | solution.py:328
  11.5 1.3 %collective-permute-start.6 = (f32[144,128]{1,0:T(8,128)S(1)}, f32[144,128]{1,0:T(8,128)S(1)}, u32[]{:S(2)}, u32[]{:S(2)}) collective-permute-start(f32[144,128]{1,0:T(8,128)S(1)} %collective-permute-done.5.refs_4_), channel_id=1, source_target_pairs={{0,4},{4,0},{8,12},{12,8},{16,20},{20,16},{24,28},{28,24},{1,5},{5... | collective-permute-start | bytes 221192 | tf_op jit(solution)/shard_map/ppermute | solution.py:328
  11.5 1.4 %collective-permute-start.8 = (f32[144,128]{1,0:T(8,128)S(1)}, f32[144,128]{1,0:T(8,128)S(1)}, u32[]{:S(2)}, u32[]{:S(2)}) collective-permute-start(f32[144,128]{1,0:T(8,128)S(1)} %collective-permute-done.7.refs_6_), channel_id=1, source_target_pairs={{0,4},{4,0},{8,12},{12,8},{16,20},{20,16},{24,28},{28,24},{1,5},{5... | collective-permute-start | bytes 221192 | tf_op jit(solution)/shard_map/ppermute | solution.py:328
  13.3 5.5 %collective-permute-start.10 = (f32[30,8,128]{2,1,0:T(8,128)S(1)}, f32[30,8,128]{2,1,0:T(8,128)S(1)}, u32[]{:S(2)}, u32[]{:S(2)}) collective-permute-start(f32[30,8,128]{2,1,0:T(8,128)S(1)} %get-tuple-element.35), channel_id=1, source_target_pairs={{0,4},{4,0},{8,12},{12,8},{16,20},{20,16},{24,28},{28,24},{1,2},{5... | collective-permute-start | bytes 368648 | tf_op jit(solution)/shard_map/ppermute | solution.py:413
  13.7 6.4 %collective-permute-start.9 = (f32[30,8,128]{2,1,0:T(8,128)S(1)}, f32[30,8,128]{2,1,0:T(8,128)S(1)}, u32[]{:S(2)}, u32[]{:S(2)}) collective-permute-start(f32[30,8,128]{2,1,0:T(8,128)S(1)} %get-tuple-element.34), channel_id=1, source_target_pairs={{0,1},{4,5},{8,9},{12,13},{16,17},{20,21},{24,25},{28,29},{1,0},{5... | collective-permute-start | bytes 368648 | tf_op jit(solution)/shard_map/ppermute | solution.py:412
  23.5 1.4 %collective-permute-start.11 = (f32[4,64,128]{2,1,0:T(8,128)S(1)}, f32[4,64,128]{2,1,0:T(8,128)S(1)}, u32[]{:S(2)}, u32[]{:S(2)}) collective-permute-start(f32[4,64,128]{2,1,0:T(8,128)S(1)} %dynamic-slice_bitcast_fusion), channel_id=1, source_target_pairs={{0,4},{4,0},{8,12},{12,8},{16,20},{20,16},{24,28},{28,24},{1,5},{5... | collective-permute-start | bytes 393224 | tf_op jit(solution)/shard_map/ppermute | solution.py:343
  25.0 4.3 %collective-permute-start.12 = (f32[64,128]{1,0:T(8,128)S(1)}, f32[64,128]{1,0:T(8,128)S(1)}, u32[]{:S(2)}, u32[]{:S(2)}) collective-permute-start(f32[64,128]{1,0:T(8,128)S(1)} %get-tuple-element.40), channel_id=1, source_target_pairs={{0,8},{4,12},{8,0},{12,4},{16,24},{20,28},{24,16},{28,20},{1,9},{5... | collective-permute-start | bytes 98312 | tf_op jit(solution)/shard_map/ppermute | solution.py:343
  25.6 4.3 %collective-permute-start.13 = (f32[64,128]{1,0:T(8,128)S(1)}, f32[64,128]{1,0:T(8,128)S(1)}, u32[]{:S(2)}, u32[]{:S(2)}) collective-permute-start(f32[64,128]{1,0:T(8,128)S(1)} %get-tuple-element.42), channel_id=1, source_target_pairs={{0,16},{4,20},{8,24},{12,28},{16,0},{20,4},{24,8},{28,12},{1,17},{... | collective-permute-start | bytes 98312 | tf_op jit(solution)/shard_map/ppermute | solution.py:343
  26.3 4.8 %collective-permute-start.14 = (f32[64,128]{1,0:T(8,128)S(1)}, f32[64,128]{1,0:T(8,128)S(1)}, u32[]{:S(2)}, u32[]{:S(2)}) collective-permute-start(f32[64,128]{1,0:T(8,128)S(1)} %get-tuple-element.41), channel_id=1, source_target_pairs={{0,24},{4,28},{8,16},{12,20},{16,8},{20,12},{24,0},{28,4},{1,25},{... | collective-permute-start | bytes 98312 | tf_op jit(solution)/shard_map/ppermute | solution.py:343

commit v2 on v1

--- a/solution.py
+++ b/solution.py
@@ -60,11 +60,13 @@
     even = lax.rem(lax.axis_index("tile"), 2) == 0
     for d, h in enumerate(halos):
         want = wanted[d, :slabs, :]
-        hits = [want == float(k) for k in range(1, len(slices))]
-        for r in range(rows):
-            value = slices[0][tiled_row(r, slabs), :]
-            for k, hit in enumerate(hits):
-                value = jnp.where(hit, slices[k + 1][tiled_row(r, slabs), :], value)
+        values = [slices[0][tiled_row(r, slabs), :] for r in range(rows)]
+        for k in range(1, len(slices)):
+            hit = want == float(k)
+            values = [
+                jnp.where(hit, slices[k][tiled_row(r, slabs), :], v) for r, v in enumerate(values)
+            ]
+        for r, value in enumerate(values):
             speeds[d, r] = value
         a0 = jnp.where(even, rows - h, 0)
         b0 = jnp.where(even, 0, rows - h)
@@ -76,22 +78,20 @@
     return 1.0 + lax.axis_index("freq").astype(jnp.float32) * (1.0 / freqs)
 
 
-def sin_cos(x):
+def sin_cos(x, scale):
     quarter = jnp.floor(x * (2.0 / math.pi) + 0.5)
     r = x - quarter * 1.5703125
-    r = r - quarter * 4.837512969970703e-4
-    r = r - quarter * 7.549789948768648e-8
+    r = r - quarter * 4.838267948966192e-4
     z = r * r
     s = r + r * z * (-1.6666654611e-1 + z * (8.3321608736e-3 - z * 1.9515295891e-4))
-    c = 1.0 - 0.5 * z + z * z * (
-        4.166664568298827e-2 + z * (-1.388731625493765e-3 + z * 2.443315711809948e-5)
+    c = 1.0 - z * (
+        0.5
+        - z * (4.166664568298827e-2 - z * (1.388731625493765e-3 - z * 2.443315711809948e-5))
     )
     q = quarter.astype(jnp.int32)
     odd = (q & 1) == 1
-    sine = jnp.where(odd, c, s)
-    cosine = jnp.where(odd, s, c)
-    sine = jnp.where((q & 2) == 2, -sine, sine)
-    cosine = jnp.where(((q + 1) & 2) == 2, -cosine, cosine)
+    sine = jnp.where(odd, c, s) * jnp.where((q & 2) == 2, -scale, scale)
+    cosine = jnp.where(odd, s, c) * jnp.where(((q + 1) & 2) == 2, -scale, scale)
     return sine, cosine
 
 
@@ -106,9 +106,9 @@
 
         def row(i, carry, d=d):
             v = speeds[d, pl.ds(i * 4, 4)]
-            s, c = sin_cos(omega * STEP_DEPTH / v)
-            sines[d, pl.ds(i * 4, 4)] = s * depth_scale(d)
-            cosines[d, pl.ds(i * 4, 4)] = c * depth_scale(d)
+            s, c = sin_cos(omega * STEP_DEPTH / v, depth_scale(d))
+            sines[d, pl.ds(i * 4, 4)] = s
+            cosines[d, pl.ds(i * 4, 4)] = c
             ratios[d, pl.ds(i * 4, 4)] = v / omega
             return carry
 
@@ -272,12 +272,12 @@
                 v = jnp.where(even, b, a) if low else jnp.where(even, a, b)
                 v = jnp.where(at_low if low else at_high, 1.0, v)
                 e = halo - h + i if low else high0 + i
-                s, c = sin_cos(omega * STEP_DEPTH / v)
+                s, c = sin_cos(omega * STEP_DEPTH / v, scale)
                 coef[e] = v / omega
-                rotate(y, turned, e, 1, (s * scale)[None], (c * scale)[None])
+                rotate(y, turned, e, 1, s[None], c[None])
             return carry
 
-        lax.fori_loop(0, h, halo_rows, 0, unroll=3)
+        lax.fori_loop(0, h, halo_rows, 0, unroll=True)
         coef[halo:high0] = ratios[d]
         k = d * SWEEPS
         for r in range(rows):

time: 31.8 us -> 31.4 us (0.987)
  Pallas kernels: 6.43 us -> 5.97 us
    pallas_call x1, Pallas kernels: 3.44 us -> 3.01 us  [on_device(): call(functools.partial(march_kernel, freqs, tiles, halos, starts), [padde...]
where the time goes in v2:
time: 31.4 us; the launch traced here: 31.3 us
  starting transfers between devices  14.3 us (46%)
  waiting for transfers between devices  8.26 us (26%)
  Pallas kernels  5.97 us (19%)
  local copies, waits for them, and re-layouts  1.33 us (4%)
  between operations  0.8 us (3%)
  other arithmetic  0.65 us (2%)
    ppermute x11, starting transfers between devices, swap(): return lax.ppermute(value, 'freq', [(i, i ^ bits) for i in range(freqs)])  8.71 us
    ppermute x11, waiting for transfers between devices, swap(): return lax.ppermute(value, 'freq', [(i, i ^ bits) for i in range(freqs)])  6.94 us
    pallas_call x1, Pallas kernels, on_device(): call(functools.partial(march_kernel, freqs, tiles, halos, starts), [padde...  3.01 us
    ppermute x1, starting transfers between devices, on_device(): speed_a = swap_a(send_a)  2.8 us
    ppermute x2, starting transfers between devices, on_device(): field_a, field_b = (swap_a(send_a), swap_b(send_b))  2.33 us
    ppermute x1, waiting for transfers between devices, on_device(): speed_a = swap_a(send_a)  1.32 us
    pallas_call x1, Pallas kernels, on_device(): call(functools.partial(prepare_kernel, halo), [(4, rows) + row, (4, halo)...  1.06 us
    pallas_call x1, Pallas kernels, on_device(): call(functools.partial(begin_kernel, freqs, tiles, halos), [padded] * 3 +...  1.02 us
  transfers between devices with their start and end apart: 15, of which 8 were waited for; matrix products, arithmetic and copies ran while one was open for 4% of the time, Pallas kernels for 6%

profile of v2, /device:TPU:0, one launch (start us, length us, event | category | flops | bytes accessed | tf_op | source)
XLA Modules:
  0.0 31.3 jit_solution(12547187759076947781)
XLA Ops:
  0.6 1.1 %shard_map.68 = (f32[4,16,8,128]{3,2,1,0:T(8,128)S(1)}, f32[4,12,8,128]{3,2,1,0:T(8,128)S(1)}, f32[4,12,8,128]{3,2,1,0:T(8,128)S(1)}, f32[144,128]{1,0:T(8,128)S(1)}, f32[4,8,128]{2,1,0:T(8,128)S(1)}) custom-call(s32[4]{0:T(128)} %owner.1, f32[2,128,128]{2,1,0:T(8,128)} %bitcast.77, f32[2,128,128]{2,1,0:T(8,128)} %bitcast.78, f32[128,128]{1,0:T(8,128)} %bitcast.79, ...), custom_call_target="tpu_custom_call" | custom-call | tf_op jit(solution)/shard_map/pallas_call | solution.py:391
  1.7 3.0 %collective-permute-start.3 = (f32[144,128]{1,0:T(8,128)S(1)}, f32[144,128]{1,0:T(8,128)S(1)}, u32[]{:S(2)}, u32[]{:S(2)}) collective-permute-start(f32[144,128]{1,0:T(8,128)S(1)} %get-tuple-element.25.refs_0_), channel_id=1, source_target_pairs={{0,8},{4,12},{8,0},{12,4},{16,24},{20,28},{24,16},{28,20},{1,9},{5... | collective-permute-start | bytes 221192 | tf_op jit(solution)/shard_map/ppermute | solution.py:328
  4.7 1.5 %collective-permute-start.5 = (f32[144,128]{1,0:T(8,128)S(1)}, f32[144,128]{1,0:T(8,128)S(1)}, u32[]{:S(2)}, u32[]{:S(2)}) collective-permute-start(f32[144,128]{1,0:T(8,128)S(1)} %get-tuple-element.25.refs_0_), channel_id=1, source_target_pairs={{0,16},{4,20},{8,24},{12,28},{16,0},{20,4},{24,8},{28,12},{1,17},{... | collective-permute-start | bytes 221192 | tf_op jit(solution)/shard_map/ppermute | solution.py:328
  6.3 0.0 collective-permute-start.7
  6.3 0.0 collective-permute-start.2
  6.3 2.0 %collective-permute-start = (f32[4,12,8,128]{3,2,1,0:T(8,128)S(1)}, f32[4,12,8,128]{3,2,1,0:T(8,128)S(1)}, u32[]{:S(2)}, u32[]{:S(2)}) collective-permute-start(f32[4,12,8,128]{3,2,1,0:T(8,128)S(1)} %get-tuple-element.22), channel_id=1, source_target_pairs={{0,1},{4,5},{8,9},{12,13},{16,17},{20,21},{24,25},{28,29},{1,0},{5... | collective-permute-start | bytes 589832 | tf_op jit(solution)/shard_map/ppermute | solution.py:404
  8.3 0.0 collective-permute-done.3.refs_2_
  8.3 0.3 collective-permute-start.1
  8.6 0.5 %collective-permute-done.5.refs_4_ = f32[144,128]{1,0:T(8,128)S(1)} collective-permute-done((f32[144,128]{1,0:T(8,128)S(1)}, f32[144,128]{1,0:T(8,128)S(1)}, u32[]{:S(2)}, u32[]{:S(2)}) %collective-permute-start.5) | collective-permute-done | bytes 73760 | tf_op jit(solution)/shard_map/ppermute | solution.py:328
  9.1 0.0 collective-permute-start.4
  9.1 2.4 %collective-permute-done.7.refs_6_ = f32[144,128]{1,0:T(8,128)S(1)} collective-permute-done((f32[144,128]{1,0:T(8,128)S(1)}, f32[144,128]{1,0:T(8,128)S(1)}, u32[]{:S(2)}, u32[]{:S(2)}) %collective-permute-start.7) | collective-permute-done | bytes 73760 | tf_op jit(solution)/shard_map/ppermute | solution.py:328
  11.5 0.0 collective-permute-start.6
  11.5 0.0 collective-permute-done.2.refs_1_
  11.5 0.5 %collective-permute-start.8 = (f32[144,128]{1,0:T(8,128)S(1)}, f32[144,128]{1,0:T(8,128)S(1)}, u32[]{:S(2)}, u32[]{:S(2)}) collective-permute-start(f32[144,128]{1,0:T(8,128)S(1)} %collective-permute-done.7.refs_6_), channel_id=1, source_target_pairs={{0,4},{4,0},{8,12},{12,8},{16,20},{20,16},{24,28},{28,24},{1,5},{5... | collective-permute-start | bytes 221192 | tf_op jit(solution)/shard_map/ppermute | solution.py:328
  12.0 0.0 collective-permute-done.4.refs_3_
  12.0 0.7 %collective-permute-done.6.refs_5_ = f32[144,128]{1,0:T(8,128)S(1)} collective-permute-done((f32[144,128]{1,0:T(8,128)S(1)}, f32[144,128]{1,0:T(8,128)S(1)}, u32[]{:S(2)}, u32[]{:S(2)}) %collective-permute-start.6) | collective-permute-done | bytes 73760 | tf_op jit(solution)/shard_map/ppermute | solution.py:328
  12.8 0.2 collective-permute-done.8.refs_7_
  12.9 0.3 shard_map.69
  13.2 0.4 %collective-permute-start.10 = (f32[30,8,128]{2,1,0:T(8,128)S(1)}, f32[30,8,128]{2,1,0:T(8,128)S(1)}, u32[]{:S(2)}, u32[]{:S(2)}) collective-permute-start(f32[30,8,128]{2,1,0:T(8,128)S(1)} %get-tuple-element.35), channel_id=1, source_target_pairs={{0,4},{4,0},{8,12},{12,8},{16,20},{20,16},{24,28},{28,24},{1,2},{5... | collective-permute-start | bytes 368648 | tf_op jit(solution)/shard_map/ppermute | solution.py:413
  13.7 2.8 %collective-permute-start.9 = (f32[30,8,128]{2,1,0:T(8,128)S(1)}, f32[30,8,128]{2,1,0:T(8,128)S(1)}, u32[]{:S(2)}, u32[]{:S(2)}) collective-permute-start(f32[30,8,128]{2,1,0:T(8,128)S(1)} %get-tuple-element.34), channel_id=1, source_target_pairs={{0,1},{4,5},{8,9},{12,13},{16,17},{20,21},{24,25},{28,29},{1,0},{5... | collective-permute-start | bytes 368648 | tf_op jit(solution)/shard_map/ppermute | solution.py:412
  16.5 0.6 %gather_fusion = f32[8,16,128]{2,1,0:T(8,128)S(1)} fusion(f32[8,16,128]{2,1,0:T(8,128)S(1)} %constant_dynamic-update-slice_fusion, s32[1024]{0:T(1024)S(1)} %pad_clamp_fusion), kind=kCustom, calls=%fused_computation | custom fusion | bytes 131104 | tf_op jit(solution)/shard_map/gather | solution.py:416
  17.1 0.6 %shard_map.70 = (f32[4,16,8,128]{3,2,1,0:T(8,128)S(1)}, f32[4,16,8,128]{3,2,1,0:T(8,128)S(1)}, f32[4,16,8,128]{3,2,1,0:T(8,128)S(1)}, f32[16,8,128]{2,1,0:T(8,128)S(1)}, f32[16,8,128]{2,1,0:T(8,128)S(1)}) custom-call(f32[4,16,8,128]{3,2,1,0:T(8,128)S(1)} %get-tuple-element.26.speeds, f32[16,8,128]{2,1,0:T(8,128)S(1)} %bitcast.74), custom_call_target="tpu_custom_call" | custom-call | tf_op jit(solution)/shard_map/pallas_call | solution.py:419
  17.6 0.0 collective-permute-done.field_a
  17.7 0.0 collective-permute-done.1.field_b
  17.7 1.0 %shard_map.71 = (f32[4,40,24,128]{3,2,1,0:T(8,128)S(1)}, f32[4,40,24,128]{3,2,1,0:T(8,128)S(1)}, f32[4,40,24,128]{3,2,1,0:T(8,128)S(1)}, f32[4,16,8,128]{3,2,1,0:T(8,128)S(1)}) custom-call(f32[4,16,8,128]{3,2,1,0:T(8,128)S(1)} %get-tuple-element.21.own, f32[4,12,8,128]{3,2,1,0:T(8,128)S(1)} %collective-permute-done.field_a, ...), custom_call_target="tpu_custom_call" | custom-call | tf_op jit(solution)/shard_map/pallas_call | solution.py:428
  18.7 0.0 collective-permute-done.10.speed_b
  18.7 1.3 %collective-permute-done.9.speed_a = f32[30,8,128]{2,1,0:T(8,128)S(1)} collective-permute-done((f32[30,8,128]{2,1,0:T(8,128)S(1)}, f32[30,8,128]{2,1,0:T(8,128)S(1)}, u32[]{:S(2)}, u32[]{:S(2)}) %collective-permute-start.9) | collective-permute-done | bytes 122912 | tf_op jit(solution)/shard_map/ppermute | solution.py:412
  20.0 3.0 %shard_map.72 = (f32[4,40,24,128]{3,2,1,0:T(8,128)S(1)}, f32[4,40,24,128]{3,2,1,0:T(8,128)S(1)}, f32[4,40,24,128]{3,2,1,0:T(8,128)S(1)}, f32[4,128,128]{2,1,0:T(8,128)S(1)}, f32[512,128]{1,0:T(8,128)S(1)}) custom-call(f32[4,40,24,128]{3,2,1,0:T(8,128)S(1)} %get-tuple-element.30.x_in, ...), custom_call_target="tpu_custom_call", output_to_operand_aliasing={{0}: (0, {}), {1}: (1, {}), {2}: (2, {})} | custom-call | tf_op jit(solution)/shard_map/pallas_call | solution.py:434
  23.1 0.1 collective-permute-start.11
  23.2 1.3 %collective-permute-done.11 = f32[4,64,128]{2,1,0:T(8,128)S(1)} collective-permute-done((f32[4,64,128]{2,1,0:T(8,128)S(1)}, f32[4,64,128]{2,1,0:T(8,128)S(1)}, u32[]{:S(2)}, u32[]{:S(2)}) %collective-permute-start.11) | collective-permute-done | bytes 131104 | tf_op jit(solution)/shard_map/ppermute | solution.py:343
  24.5 0.6 %collective-permute-start.12 = (f32[64,128]{1,0:T(8,128)S(1)}, f32[64,128]{1,0:T(8,128)S(1)}, u32[]{:S(2)}, u32[]{:S(2)}) collective-permute-start(f32[64,128]{1,0:T(8,128)S(1)} %get-tuple-element.40), channel_id=1, source_target_pairs={{0,8},{4,12},{8,0},{12,4},{16,24},{20,28},{24,16},{28,20},{1,9},{5... | collective-permute-start | bytes 98312 | tf_op jit(solution)/shard_map/ppermute | solution.py:343
  25.1 0.7 %collective-permute-start.13 = (f32[64,128]{1,0:T(8,128)S(1)}, f32[64,128]{1,0:T(8,128)S(1)}, u32[]{:S(2)}, u32[]{:S(2)}) collective-permute-start(f32[64,128]{1,0:T(8,128)S(1)} %get-tuple-element.42), channel_id=1, source_target_pairs={{0,16},{4,20},{8,24},{12,28},{16,0},{20,4},{24,8},{28,12},{1,17},{... | collective-permute-start | bytes 98312 | tf_op jit(solution)/shard_map/ppermute | solution.py:343
  25.8 2.3 %collective-permute-start.14 = (f32[64,128]{1,0:T(8,128)S(1)}, f32[64,128]{1,0:T(8,128)S(1)}, u32[]{:S(2)}, u32[]{:S(2)}) collective-permute-start(f32[64,128]{1,0:T(8,128)S(1)} %get-tuple-element.41), channel_id=1, source_target_pairs={{0,24},{4,28},{8,16},{12,20},{16,8},{20,12},{24,0},{28,4},{1,25},{... | collective-permute-start | bytes 98312 | tf_op jit(solution)/shard_map/ppermute | solution.py:343
  28.1 0.7 %copy.23 = f32[2,2,1,16,1024]{4,3,2,1,0:T(8,128)} copy(f32[2,2,1,16,1024]{4,3,2,1,0:T(8,128)S(1)} %bitcast.73) | data formatting | bytes 524288
  28.8 0.0 collective-permute-done.12
  28.8 0.6 %collective-permute-done.13 = f32[64,128]{1,0:T(8,128)S(1)} collective-permute-done((f32[64,128]{1,0:T(8,128)S(1)}, f32[64,128]{1,0:T(8,128)S(1)}, u32[]{:S(2)}, u32[]{:S(2)}) %collective-permute-start.13) | collective-permute-done | bytes 32800 | tf_op jit(solution)/shard_map/ppermute | solution.py:343
  29.4 1.2 %collective-permute-done.14 = f32[64,128]{1,0:T(8,128)S(1)} collective-permute-done((f32[64,128]{1,0:T(8,128)S(1)}, f32[64,128]{1,0:T(8,128)S(1)}, u32[]{:S(2)}, u32[]{:S(2)}) %collective-permute-start.14) | collective-permute-done | bytes 32800 | tf_op jit(solution)/shard_map/ppermute | solution.py:343
  30.6 0.6 %fusion.1 = f32[64,128]{1,0:T(8,128)} fusion(f32[64,128]{1,0:T(8,128)S(1)} %collective-permute-done.14, f32[64,128]{1,0:T(8,128)S(1)} %collective-permute-done.13, f32[64,128]{1,0:T(8,128)S(1)} %collective-permute-done.12, f32[4,64,128]{2,1,0:T(8,128)S(1)} %bitcast_add_fusion, s32[]{:T(128)S(6)} %select_n.39), kind=kLoop, calls=%fused_computation.6 | loop fusion | flops 24576 | bytes 163844 | tf_op jit(solution)/shard_map/add | solution.py:354
  (14 shorter events, 0.1 us)
Async XLA Ops:
  1.7 6.6 %collective-permute-start.3 = (f32[144,128]{1,0:T(8,128)S(1)}, f32[144,128]{1,0:T(8,128)S(1)}, u32[]{:S(2)}, u32[]{:S(2)}) collective-permute-start(f32[144,128]{1,0:T(8,128)S(1)} %get-tuple-element.25.refs_0_), channel_id=1, source_target_pairs={{0,8},{4,12},{8,0},{12,4},{16,24},{20,28},{24,16},{28,20},{1,9},{5... | collective-permute-start | bytes 221192 | tf_op jit(solution)/shard_map/ppermute | solution.py:328
  4.7 4.4 %collective-permute-start.5 = (f32[144,128]{1,0:T(8,128)S(1)}, f32[144,128]{1,0:T(8,128)S(1)}, u32[]{:S(2)}, u32[]{:S(2)}) collective-permute-start(f32[144,128]{1,0:T(8,128)S(1)} %get-tuple-element.25.refs_0_), channel_id=1, source_target_pairs={{0,16},{4,20},{8,24},{12,28},{16,0},{20,4},{24,8},{28,12},{1,17},{... | collective-permute-start | bytes 221192 | tf_op jit(solution)/shard_map/ppermute | solution.py:328
  6.3 5.3 %collective-permute-start.7 = (f32[144,128]{1,0:T(8,128)S(1)}, f32[144,128]{1,0:T(8,128)S(1)}, u32[]{:S(2)}, u32[]{:S(2)}) collective-permute-start(f32[144,128]{1,0:T(8,128)S(1)} %get-tuple-element.25.refs_0_), channel_id=1, source_target_pairs={{0,24},{4,28},{8,16},{12,20},{16,8},{20,12},{24,0},{28,4},{1,25},{... | collective-permute-start | bytes 221192 | tf_op jit(solution)/shard_map/ppermute | solution.py:328
  6.3 5.2 %collective-permute-start.2 = (f32[144,128]{1,0:T(8,128)S(1)}, f32[144,128]{1,0:T(8,128)S(1)}, u32[]{:S(2)}, u32[]{:S(2)}) collective-permute-start(f32[144,128]{1,0:T(8,128)S(1)} %get-tuple-element.25.refs_0_), channel_id=1, source_target_pairs={{0,4},{4,0},{8,12},{12,8},{16,20},{20,16},{24,28},{28,24},{1,5},{5... | collective-permute-start | bytes 221192 | tf_op jit(solution)/shard_map/ppermute | solution.py:328
  6.3 11.4 %collective-permute-start = (f32[4,12,8,128]{3,2,1,0:T(8,128)S(1)}, f32[4,12,8,128]{3,2,1,0:T(8,128)S(1)}, u32[]{:S(2)}, u32[]{:S(2)}) collective-permute-start(f32[4,12,8,128]{3,2,1,0:T(8,128)S(1)} %get-tuple-element.22), channel_id=1, source_target_pairs={{0,1},{4,5},{8,9},{12,13},{16,17},{20,21},{24,25},{28,29},{1,0},{5... | collective-permute-start | bytes 589832 | tf_op jit(solution)/shard_map/ppermute | solution.py:404
  8.3 9.3 %collective-permute-start.1 = (f32[4,12,8,128]{3,2,1,0:T(8,128)S(1)}, f32[4,12,8,128]{3,2,1,0:T(8,128)S(1)}, u32[]{:S(2)}, u32[]{:S(2)}) collective-permute-start(f32[4,12,8,128]{3,2,1,0:T(8,128)S(1)} %get-tuple-element.23), channel_id=1, source_target_pairs={{0,4},{4,0},{8,12},{12,8},{16,20},{20,16},{24,28},{28,24},{1,2},{5... | collective-permute-start | bytes 589832 | tf_op jit(solution)/shard_map/ppermute | solution.py:404
  9.1 2.9 %collective-permute-start.4 = (f32[144,128]{1,0:T(8,128)S(1)}, f32[144,128]{1,0:T(8,128)S(1)}, u32[]{:S(2)}, u32[]{:S(2)}) collective-permute-start(f32[144,128]{1,0:T(8,128)S(1)} %collective-permute-done.3.refs_2_), channel_id=1, source_target_pairs={{0,4},{4,0},{8,12},{12,8},{16,20},{20,16},{24,28},{28,24},{1,5},{5... | collective-permute-start | bytes 221192 | tf_op jit(solution)/shard_map/ppermute | solution.py:328
  11.5 1.3 %collective-permute-start.6 = (f32[144,128]{1,0:T(8,128)S(1)}, f32[144,128]{1,0:T(8,128)S(1)}, u32[]{:S(2)}, u32[]{:S(2)}) collective-permute-start(f32[144,128]{1,0:T(8,128)S(1)} %collective-permute-done.5.refs_4_), channel_id=1, source_target_pairs={{0,4},{4,0},{8,12},{12,8},{16,20},{20,16},{24,28},{28,24},{1,5},{5... | collective-permute-start | bytes 221192 | tf_op jit(solution)/shard_map/ppermute | solution.py:328
  11.5 1.4 %collective-permute-start.8 = (f32[144,128]{1,0:T(8,128)S(1)}, f32[144,128]{1,0:T(8,128)S(1)}, u32[]{:S(2)}, u32[]{:S(2)}) collective-permute-start(f32[144,128]{1,0:T(8,128)S(1)} %collective-permute-done.7.refs_6_), channel_id=1, source_target_pairs={{0,4},{4,0},{8,12},{12,8},{16,20},{20,16},{24,28},{28,24},{1,5},{5... | collective-permute-start | bytes 221192 | tf_op jit(solution)/shard_map/ppermute | solution.py:328
  13.2 5.4 %collective-permute-start.10 = (f32[30,8,128]{2,1,0:T(8,128)S(1)}, f32[30,8,128]{2,1,0:T(8,128)S(1)}, u32[]{:S(2)}, u32[]{:S(2)}) collective-permute-start(f32[30,8,128]{2,1,0:T(8,128)S(1)} %get-tuple-element.35), channel_id=1, source_target_pairs={{0,4},{4,0},{8,12},{12,8},{16,20},{20,16},{24,28},{28,24},{1,2},{5... | collective-permute-start | bytes 368648 | tf_op jit(solution)/shard_map/ppermute | solution.py:413
  13.7 6.4 %collective-permute-start.9 = (f32[30,8,128]{2,1,0:T(8,128)S(1)}, f32[30,8,128]{2,1,0:T(8,128)S(1)}, u32[]{:S(2)}, u32[]{:S(2)}) collective-permute-start(f32[30,8,128]{2,1,0:T(8,128)S(1)} %get-tuple-element.34), channel_id=1, source_target_pairs={{0,1},{4,5},{8,9},{12,13},{16,17},{20,21},{24,25},{28,29},{1,0},{5... | collective-permute-start | bytes 368648 | tf_op jit(solution)/shard_map/ppermute | solution.py:412
  23.1 1.4 %collective-permute-start.11 = (f32[4,64,128]{2,1,0:T(8,128)S(1)}, f32[4,64,128]{2,1,0:T(8,128)S(1)}, u32[]{:S(2)}, u32[]{:S(2)}) collective-permute-start(f32[4,64,128]{2,1,0:T(8,128)S(1)} %dynamic-slice_bitcast_fusion), channel_id=1, source_target_pairs={{0,4},{4,0},{8,12},{12,8},{16,20},{20,16},{24,28},{28,24},{1,5},{5... | collective-permute-start | bytes 393224 | tf_op jit(solution)/shard_map/ppermute | solution.py:343
  24.5 4.3 %collective-permute-start.12 = (f32[64,128]{1,0:T(8,128)S(1)}, f32[64,128]{1,0:T(8,128)S(1)}, u32[]{:S(2)}, u32[]{:S(2)}) collective-permute-start(f32[64,128]{1,0:T(8,128)S(1)} %get-tuple-element.40), channel_id=1, source_target_pairs={{0,8},{4,12},{8,0},{12,4},{16,24},{20,28},{24,16},{28,20},{1,9},{5... | collective-permute-start | bytes 98312 | tf_op jit(solution)/shard_map/ppermute | solution.py:343
  25.1 4.3 %collective-permute-start.13 = (f32[64,128]{1,0:T(8,128)S(1)}, f32[64,128]{1,0:T(8,128)S(1)}, u32[]{:S(2)}, u32[]{:S(2)}) collective-permute-start(f32[64,128]{1,0:T(8,128)S(1)} %get-tuple-element.42), channel_id=1, source_target_pairs={{0,16},{4,20},{8,24},{12,28},{16,0},{20,4},{24,8},{28,12},{1,17},{... | collective-permute-start | bytes 98312 | tf_op jit(solution)/shard_map/ppermute | solution.py:343
  25.8 4.8 %collective-permute-start.14 = (f32[64,128]{1,0:T(8,128)S(1)}, f32[64,128]{1,0:T(8,128)S(1)}, u32[]{:S(2)}, u32[]{:S(2)}) collective-permute-start(f32[64,128]{1,0:T(8,128)S(1)} %get-tuple-element.41), channel_id=1, source_target_pairs={{0,24},{4,28},{8,16},{12,20},{16,8},{20,12},{24,0},{28,4},{1,25},{... | collective-permute-start | bytes 98312 | tf_op jit(solution)/shard_map/ppermute | solution.py:343
